TPU v7x, 128 devices: a whole 4x4x4 slice. The times are simulated.
128 devices in a mesh: gx: 16 (over y, x), gy: 8 (over z, core).
Axes of the slice: x: 4, y: 4, z: 4, core: 2. Of those that a mesh axis runs over, the one named last changes fastest.
Arguments:
- matrix_pressure: float32 [2048, 2048], P('gx', 'gy'), may hold values from 0 to 1
- permeability: float32 [2048, 2048], P('gx', 'gy'), may hold values from 0.2 to 5
- matrix_storage: float32 [2048, 2048], P('gx', 'gy'), may hold values from 0.5 to 2
- fracture_pressure: float32 [512, 128, 128], P(('gx', 'gy')), may hold values from 0 to 0.4
- initial_aperture: float32 [512, 128, 128], P(('gx', 'gy')), may hold values from 0.6 to 2
- normal_stress: float32 [512, 128, 128], P(('gx', 'gy')), may hold values from 0.5 to 4
- isect_cell: int32 [524288], P(('gx', 'gy')), may hold values from 0 to 32767
- isect_owner: int32 [524288, 1], P(('gx', 'gy')), may hold values from 0 to 127; in each aligned block of 4096 rows (0 to 4095, 4096 to 8191, ...) at most 64 rows name the same one
- isect_frac: int32 [524288], P(('gx', 'gy')), may hold values from 0 to 3
- isect_seg: int32 [524288], P(('gx', 'gy')), may hold values from 0 to 16383
- well_index: float32 [524288], P(('gx', 'gy')), may hold values from 0.5 to 5
- junc_frac: int32 [262144], P(('gx', 'gy')), may hold values from 0 to 3
- junc_seg: int32 [262144], P(('gx', 'gy')), may hold values from 0 to 16383
- junc_owner: int32 [262144, 1], P(('gx', 'gy')), may hold values from 0 to 127; in each aligned block of 2048 rows (0 to 2047, 2048 to 4095, ...) at most 32 rows name the same one
- junc_far_frac: int32 [262144], P(('gx', 'gy')), may hold values from 0 to 3
- junc_far_seg: int32 [262144], P(('gx', 'gy')), may hold values from 0 to 16383
- junc_trans: float32 [262144], P(('gx', 'gy')), may hold values from 0.5 to 5
Outputs:
- fracture_new: float32 [512, 128, 128], P(('gx', 'gy'))
- matrix_new: float32 [2048, 2048], P('gx', 'gy')
Inputs may be any that keep to these rules, and one draw needn't show every extreme that they name: `isect_owner`: in the rows of one device no owner is named by more than 64 rows, and some owner reaches 64. `junc_owner`: in the rows of one device no owner is named by more than 32 rows, and some owner reaches 32.
All inputs are finite; a program needn't handle non-finite values.
Results may differ from a plain program's by a relative error of at most 0.0003.
Values sent between devices are 32-bit elements; how exact they have to be, the bound alone decides.
A program may use at most 64 MiB of HBM per device.

v0:
```python
import jax
import jax.numpy as jnp
from jax import lax
from jax.sharding import PartitionSpec as P

SWEEPS = 3


def padded_2(cells, sides, width):
    for axis, dim in sides:
        count = lax.axis_size(axis)
        ends = count - 1
        head = lax.slice_in_dim(cells, 0, width, axis=dim)
        tail = lax.slice_in_dim(cells, cells.shape[dim] - width, cells.shape[dim], axis=dim)
        cells = jnp.concatenate(
            [
                lax.ppermute(tail, axis, [(i, (i + 1) % count) for i in range(ends)]),
                cells,
                lax.ppermute(head, axis, [((i + 1) % count, i) for i in range(ends)]),
            ],
            axis=dim,
        )
    return cells


def harmonic(first, second):
    return 2.0 * first * second / (first + second)


def slot_numbers(targets, devices):
    count_rows = targets.shape[0]
    block = min(count_rows, 1024)
    blocks = targets.reshape(count_rows // block, block)
    owners = jnp.arange(devices, dtype=jnp.int32)
    row_ids = lax.broadcasted_iota(jnp.int32, (block, block), 0)
    col_ids = lax.broadcasted_iota(jnp.int32, (block, block), 1)
    lower = (col_ids < row_ids).astype(jnp.bfloat16)

    def advance(counts, part):
        matches = part[:, None] == owners[None, :]
        onehot = matches.astype(jnp.int32)
        earlier = jnp.dot(
            lower, matches.astype(jnp.bfloat16), preferred_element_type=jnp.float32
        ).astype(jnp.int32)
        before = earlier + counts[None, :]
        return (counts + jnp.sum(onehot, axis=0), jnp.sum(before * onehot, axis=1))

    unused, slots = lax.scan(advance, jnp.zeros((devices,), jnp.int32), blocks)
    return slots.reshape(count_rows)


def shards(
    matrix_pressure,
    permeability,
    matrix_storage,
    fracture_pressure,
    initial_aperture,
    normal_stress,
    isect_cell,
    isect_owner,
    isect_frac,
    isect_seg,
    well_index,
    junc_frac,
    junc_seg,
    junc_owner,
    junc_far_frac,
    junc_far_seg,
    junc_trans,
):
    devices = lax.axis_size(("gx", "gy"))
    frac_count, side, unused_side = fracture_pressure.shape
    rows_x, rows_y = matrix_pressure.shape
    area = side * side
    shape = fracture_pressure.shape
    capacity = 2 * isect_cell.shape[0] // devices
    targets = isect_owner[:, 0]
    position = targets * capacity + slot_numbers(targets, devices)
    slots_all = devices * capacity
    sample = (
        jnp.zeros((slots_all,), jnp.float32)
        .at[position]
        .set(matrix_pressure.reshape(-1)[isect_cell])
    )
    weight = jnp.zeros((slots_all,), jnp.float32).at[position].set(well_index)
    frac_index = jnp.zeros((slots_all,), jnp.int32).at[position].set(isect_frac * area + isect_seg)
    values = jnp.stack([sample, weight])
    got_values, got_index = (
        lax.all_to_all(
            values.reshape(2, devices, capacity),
            ("gx", "gy"),
            split_axis=1,
            concat_axis=1,
            tiled=True,
        ),
        lax.all_to_all(
            frac_index.reshape(1, devices, capacity),
            ("gx", "gy"),
            split_axis=1,
            concat_axis=1,
            tiled=True,
        ),
    )
    got_values = got_values.reshape(2, slots_all)
    got_index = got_index.reshape(slots_all)
    source_diag = jnp.zeros((frac_count * area,), jnp.float32).at[got_index].add(got_values[1])
    source_rhs = (
        jnp.zeros((frac_count * area,), jnp.float32)
        .at[got_index]
        .add(got_values[1] * got_values[0])
    )
    effective = normal_stress - fracture_pressure
    aperture = initial_aperture - 0.5 * effective / (0.5 + effective)
    conduct = aperture * aperture * aperture
    face_rows = harmonic(conduct[:, 1:, :], conduct[:, :-1, :])
    face_cols = harmonic(conduct[:, :, 1:], conduct[:, :, :-1])
    north = jnp.pad(face_rows, ((0, 0), (1, 0), (0, 0)))
    south = jnp.pad(face_rows, ((0, 0), (0, 1), (0, 0)))
    west = jnp.pad(face_cols, ((0, 0), (0, 0), (1, 0)))
    east = jnp.pad(face_cols, ((0, 0), (0, 0), (0, 1)))
    junc_cap = 2 * junc_frac.shape[0] // devices
    junc_targets = junc_owner[:, 0]
    junc_position = junc_targets * junc_cap + slot_numbers(junc_targets, devices)
    requests = (
        jnp.zeros((devices * junc_cap,), jnp.int32)
        .at[junc_position]
        .set(junc_far_frac * area + junc_far_seg)
    )
    served = lax.all_to_all(
        requests.reshape(devices, junc_cap), ("gx", "gy"), split_axis=0, concat_axis=0, tiled=True
    )
    near_flat = junc_frac * area + junc_seg
    junc_diag = jnp.zeros((frac_count * area,), jnp.float32).at[near_flat].add(junc_trans)
    denom = (
        aperture
        + north
        + south
        + west
        + east
        + source_diag.reshape(shape)
        + junc_diag.reshape(shape)
    )
    stored = aperture * fracture_pressure + source_rhs.reshape(shape)
    current = fracture_pressure
    for sweep in range(SWEEPS):
        answer = current.reshape(-1)[served]
        returned = lax.all_to_all(answer, ("gx", "gy"), split_axis=0, concat_axis=0, tiled=True)
        partner = returned.reshape(-1)[junc_position]
        junc_rhs = (
            jnp.zeros((frac_count * area,), jnp.float32).at[near_flat].add(junc_trans * partner)
        )
        padded = jnp.pad(current, ((0, 0), (1, 1), (1, 1)))
        total = stored + north * padded[:, :-2, 1:-1] + south * padded[:, 2:, 1:-1]
        total = (
            total
            + west * padded[:, 1:-1, :-2]
            + east * padded[:, 1:-1, 2:]
            + junc_rhs.reshape(shape)
        )
        current = total / denom
    reply = current.reshape(-1)[got_index]
    back_values = lax.all_to_all(
        reply.reshape(devices, capacity), ("gx", "gy"), split_axis=0, concat_axis=0, tiled=True
    )
    at_fracture = back_values.reshape(-1)[position]
    m_diag = (
        jnp.zeros((rows_x * rows_y,), jnp.float32)
        .at[isect_cell]
        .add(well_index)
        .reshape(rows_x, rows_y)
    )
    m_rhs = (
        jnp.zeros((rows_x * rows_y,), jnp.float32)
        .at[isect_cell]
        .add(well_index * at_fracture)
        .reshape(rows_x, rows_y)
    )
    fields = jnp.stack([matrix_pressure, permeability])
    widened = padded_2(fields, (("gx", 1), ("gy", 2)), 1)
    total = matrix_storage * matrix_pressure + m_rhs
    weights = matrix_storage + m_diag
    for a, b in ((0, 1), (2, 1), (1, 0), (1, 2)):
        face = harmonic(permeability, widened[1, a : a + rows_x, b : b + rows_y])
        total = total + face * widened[0, a : a + rows_x, b : b + rows_y]
        weights = weights + face
    matrix_new = total / weights
    return (current, matrix_new)


def solution(mesh):
    in_specs = (
        P("gx", "gy"),
        P("gx", "gy"),
        P("gx", "gy"),
        P(("gx", "gy"), None, None),
        P(("gx", "gy"), None, None),
        P(("gx", "gy"), None, None),
        P(("gx", "gy")),
        P(("gx", "gy"), None),
        P(("gx", "gy")),
        P(("gx", "gy")),
        P(("gx", "gy")),
        P(("gx", "gy")),
        P(("gx", "gy")),
        P(("gx", "gy"), None),
        P(("gx", "gy")),
        P(("gx", "gy")),
        P(("gx", "gy")),
    )
    out_specs = (P(("gx", "gy"), None, None), P("gx", "gy"))
    return jax.shard_map(shards, mesh=mesh, in_specs=in_specs, out_specs=out_specs, check_vma=False)
```

profile of v0, /device:TPU:1, one launch (start us, length us, event | category | flops | bytes accessed | tf_op | source)
XLA Modules:
  0.0 560.3 jit_solution(17144828218275967043)
XLA Ops:
  1.2 1.3 reduce.29
  2.6 1.8 while.27
  4.5 8.1 %scatter_custom_fusion.4 = s32[4096]{0:T(1024)S(1)} fusion(s32[2048]{0:T(1024)S(1)} %bitcast.158, s32[2048]{0:T(1024)S(1)} %multiply_add_fusion.2, s32[]{:T(128)} %constant.25.clone.1), kind=kCustom, calls=%fused_computation.172 | custom fusion | bytes 16388 | tf_op jit(solution)/shard_map/scatter | solution.py:127
  12.6 0.7 all_to_all.40
  13.3 11.5 %all-to-all-start.2 = ((s32[128,1,32]{2,1,0:T(1,128)}), s32[128,1,32]{2,1,0:T(1,128)S(1)}, u32[]{:S(2)}, u32[]{:S(2)}) async-start(s32[128,1,32]{2,1,0:T(1,128)} %bitcast.6), calls=%async_computation.2 | async-start | bytes 131072 | tf_op jit(solution)/shard_map/all_to_all | solution.py:129
  24.8 3.3 collective-permute-start
  28.1 1.3 collective-permute-start.1
  31.1 3.6 while.26
  35.5 23.0 %gather_fusion = f32[4096]{0:T(1024)S(1)} fusion(f32[32768]{0:T(1024)S(1)} %bitcast.121, s32[4096]{0:T(1024)S(1)} %get-tuple-element.133), kind=kCustom, calls=%fused_computation | custom fusion | bytes 49152 | tf_op jit(solution)/shard_map/gather | solution.py:83
  58.6 15.5 %scatter_custom_fusion.1 = f32[8192]{0:T(1024)S(1)} fusion(s32[4096]{0:T(1024)S(1)} %bitcast.153, f32[4096]{0:T(1024)S(1)} %gather_fusion, f32[]{:T(128)} %constant.24.clone.1), kind=kCustom, calls=%fused_computation.163 | custom fusion | bytes 32772 | tf_op jit(solution)/shard_map/scatter | solution.py:83
  74.2 15.7 %scatter_custom_fusion.2 = f32[8192]{0:T(1024)S(1)} fusion(s32[4096]{0:T(1024)S(1)} %bitcast.154, f32[4096]{0:T(1024)} %param.31, f32[]{:T(128)} %constant.24.clone.1), kind=kCustom, calls=%fused_computation.161 | custom fusion | bytes 33280 | tf_op jit(solution)/shard_map/scatter | solution.py:85
  90.3 0.8 reshape.450
  91.0 15.5 %scatter_custom_fusion = s32[8192]{0:T(1024)S(1)} fusion(s32[4096]{0:T(1024)S(1)} %bitcast.155, s32[4096]{0:T(1024)S(1)} %multiply_add_fusion.1, s32[]{:T(128)} %constant.25.clone.1), kind=kCustom, calls=%fused_computation.166 | custom fusion | bytes 32772 | tf_op jit(solution)/shard_map/scatter | solution.py:86
  107.3 11.3 %scatter_custom_fusion.7 = f32[65536]{0:T(1024)S(1)} fusion(s32[2048]{0:T(1024)S(1)} %compare_select_fusion.5, f32[2048]{0:T(1024)S(1)} %copy-done.7, f32[]{:T(128)} %constant.24.clone.1), kind=kCustom, calls=%fused_computation.142 | custom fusion | flops 2048 | bytes 262148 | tf_op jit(solution)/shard_map/scatter-add | solution.py:133
  118.6 11.0 %all-to-all-start = ((s32[1,128,64]{2,0,1:T(1,128)}), s32[1,128,64]{2,0,1:T(1,128)S(1)}, u32[]{:S(2)}, u32[]{:S(2)}) async-start(s32[1,128,64]{2,0,1:T(1,128)} %bitcast.1), calls=%async_computation | async-start | bytes 131072 | tf_op jit(solution)/shard_map/all_to_all | solution.py:96
  129.8 23.0 %gather_fusion.1 = f32[4096]{0:T(1024)S(1)} fusion(f32[65536]{0:T(1024)S(1)} %bitcast.117, s32[4096]{0:T(1024)S(1)} %broadcast_clamp_fusion.2), kind=kCustom, calls=%fused_computation.1 | custom fusion | bytes 49152 | tf_op jit(solution)/shard_map/gather | solution.py:146
  152.8 0.7 all_to_all.43
  153.5 9.8 %all-to-all-start.3 = ((f32[128,1,32]{2,1,0:T(1,128)}), f32[128,1,32]{2,1,0:T(1,128)S(1)}, u32[]{:S(2)}, u32[]{:S(2)}) async-start(f32[128,1,32]{2,1,0:T(1,128)} %bitcast.8), calls=%async_computation.3 | async-start | bytes 131072 | tf_op jit(solution)/shard_map/all_to_all | solution.py:147
  163.4 0.8 reduce.32
  164.3 8.4 %all-to-all-done.3 = f32[128,1,32]{2,1,0:T(1,128)S(1)} async-done(((f32[128,1,32]{2,1,0:T(1,128)}), f32[128,1,32]{2,1,0:T(1,128)S(1)}, u32[]{:S(2)}, u32[]{:S(2)}) %all-to-all-start.3) | async-done | bytes 16416 | tf_op jit(solution)/shard_map/all_to_all | solution.py:147
  172.6 4.6 all-to-all-start.1
  177.8 0.8 reduce.30
  178.7 11.8 %gather_fusion.2 = f32[2048]{0:T(1024)S(1)} fusion(f32[4096]{0:T(1024)S(1)} %reshape.168, s32[2048]{0:T(1024)S(1)} %broadcast_clamp_fusion.4), kind=kCustom, calls=%fused_computation.2 | custom fusion | bytes 24576 | tf_op jit(solution)/shard_map/gather | solution.py:148
  190.5 11.3 %scatter_custom_fusion.5 = f32[65536]{0:T(1024)S(1)} fusion(s32[2048]{0:T(1024)S(1)} %compare_select_fusion.5, f32[2048]{0:T(1024)S(1)} %mul.169, f32[]{:T(128)} %constant.24.clone.1), kind=kCustom, calls=%fused_computation.146 | custom fusion | flops 2048 | bytes 262148 | tf_op jit(solution)/shard_map/scatter-add | solution.py:150
  202.3 0.8 reduce.36
  203.8 52.3 %scatter_custom_fusion.6 = f32[65536]{0:T(1024)S(1)} fusion(s32[8192]{0:T(1024)S(1)} %bitcast.148, f32[8192]{0:T(1024)S(1)} %reshape.306, f32[]{:T(128)} %constant.24.clone.1), kind=kCustom, calls=%fused_computation.144 | custom fusion | flops 8192 | bytes 262148 | tf_op jit(solution)/shard_map/scatter-add | solution.py:106
  256.1 52.3 %scatter_custom_fusion.3 = f32[65536]{0:T(1024)S(1)} fusion(s32[8192]{0:T(1024)S(1)} %bitcast.149, f32[8192]{0:T(1024)S(1)} %mul.152, f32[]{:T(128)} %constant.24.clone.1), kind=kCustom, calls=%fused_computation.148 | custom fusion | flops 8192 | bytes 262148 | tf_op jit(solution)/shard_map/scatter-add | solution.py:110
  308.7 23.0 %gather_fusion.3 = f32[4096]{0:T(1024)S(1)} fusion(f32[65536]{0:T(1024)S(1)} %bitcast.118, s32[4096]{0:T(1024)S(1)} %broadcast_clamp_fusion.2), kind=kCustom, calls=%fused_computation.3 | custom fusion | bytes 49152 | tf_op jit(solution)/shard_map/gather | solution.py:146
  332.4 9.0 %all-to-all-start.4 = ((f32[128,1,32]{2,1,0:T(1,128)}), f32[128,1,32]{2,1,0:T(1,128)S(1)}, u32[]{:S(2)}, u32[]{:S(2)}) async-start(f32[128,1,32]{2,1,0:T(1,128)} %bitcast.13), calls=%async_computation.4 | async-start | bytes 131072 | tf_op jit(solution)/shard_map/all_to_all | solution.py:147
  341.6 3.7 collective-permute-start.2
  345.2 1.9 collective-permute-start.3
  347.2 3.6 all-to-all-done.4
  350.8 0.8 reduce.33
  351.7 11.8 %gather_fusion.4 = f32[2048]{0:T(1024)S(1)} fusion(f32[4096]{0:T(1024)S(1)} %reshape.173, s32[2048]{0:T(1024)S(1)} %broadcast_clamp_fusion.4), kind=kCustom, calls=%fused_computation.4 | custom fusion | bytes 24576 | tf_op jit(solution)/shard_map/gather | solution.py:148
  363.5 11.3 %scatter_custom_fusion.8 = f32[65536]{0:T(1024)S(1)} fusion(s32[2048]{0:T(1024)S(1)} %compare_select_fusion.5, f32[2048]{0:T(1024)S(1)} %mul.174, f32[]{:T(128)} %constant.24.clone.1), kind=kCustom, calls=%fused_computation.140 | custom fusion | flops 2048 | bytes 262148 | tf_op jit(solution)/shard_map/scatter-add | solution.py:150
  375.2 23.0 %gather_fusion.5 = f32[4096]{0:T(1024)S(1)} fusion(f32[65536]{0:T(1024)S(1)} %bitcast.119, s32[4096]{0:T(1024)S(1)} %broadcast_clamp_fusion.2), kind=kCustom, calls=%fused_computation.5 | custom fusion | bytes 49152 | tf_op jit(solution)/shard_map/gather | solution.py:146
  398.9 6.1 %all-to-all-start.5 = ((f32[128,1,32]{2,1,0:T(1,128)}), f32[128,1,32]{2,1,0:T(1,128)S(1)}, u32[]{:S(2)}, u32[]{:S(2)}) async-start(f32[128,1,32]{2,1,0:T(1,128)} %bitcast.16), calls=%async_computation.5 | async-start | bytes 131072 | tf_op jit(solution)/shard_map/all_to_all | solution.py:147
  405.1 9.3 %all-to-all-done.5 = f32[128,1,32]{2,1,0:T(1,128)S(1)} async-done(((f32[128,1,32]{2,1,0:T(1,128)}), f32[128,1,32]{2,1,0:T(1,128)S(1)}, u32[]{:S(2)}, u32[]{:S(2)}) %all-to-all-start.5) | async-done | bytes 16416 | tf_op jit(solution)/shard_map/all_to_all | solution.py:147
  414.4 0.8 reduce.34
  415.2 11.8 %gather_fusion.6 = f32[2048]{0:T(1024)S(1)} fusion(f32[4096]{0:T(1024)S(1)} %reshape.176, s32[2048]{0:T(1024)S(1)} %broadcast_clamp_fusion.4), kind=kCustom, calls=%fused_computation.6 | custom fusion | bytes 24576 | tf_op jit(solution)/shard_map/gather | solution.py:148
  427.0 11.7 %scatter_custom_fusion.9 = f32[65536]{0:T(1024)S(1)} fusion(s32[2048]{0:T(1024)} %copy-done.22, f32[2048]{0:T(1024)S(1)} %mul.179, f32[]{:T(128)} %constant.24.clone.1), kind=kCustom, calls=%fused_computation.138 | custom fusion | flops 2048 | bytes 262656 | tf_op jit(solution)/shard_map/scatter-add | solution.py:150
  439.1 45.5 %gather_fusion.7 = f32[8192]{0:T(1024)S(1)} fusion(f32[65536]{0:T(1024)S(1)} %bitcast.120, s32[8192]{0:T(1024)S(1)} %broadcast_clamp_fusion), kind=kCustom, calls=%fused_computation.7 | custom fusion | bytes 98304 | tf_op jit(solution)/shard_map/gather | solution.py:161
  485.4 4.6 all-to-all-start.6
  490.0 22.1 %scatter_custom_fusion.11 = f32[32768]{0:T(1024)S(1)} fusion(s32[4096]{0:T(1024)} %get-tuple-element.132, f32[4096]{0:T(1024)S(1)} %copy-done.13, f32[]{:T(128)} %constant.24.clone.1), kind=kCustom, calls=%fused_computation.153 | custom fusion | flops 4096 | bytes 131584 | tf_op jit(solution)/shard_map/scatter-add | solution.py:169
  512.1 0.8 reduce.35
  513.0 23.0 %gather_fusion.8 = f32[4096]{0:T(1024)S(1)} fusion(f32[8192]{0:T(1024)S(1)} %reshape.179, s32[4096]{0:T(1024)S(1)} %broadcast_clamp_fusion.1), kind=kCustom, calls=%fused_computation.8 | custom fusion | bytes 49152 | tf_op jit(solution)/shard_map/gather | solution.py:165
  536.1 22.2 %scatter_custom_fusion.10 = f32[32768]{0:T(1024)S(1)} fusion(s32[4096]{0:T(1024)} %get-tuple-element.132, f32[4096]{0:T(1024)S(1)} %mul.181, f32[]{:T(128)} %constant.24.clone.1), kind=kCustom, calls=%fused_computation.155 | custom fusion | flops 4096 | bytes 131584 | tf_op jit(solution)/shard_map/scatter-add | solution.py:175
  558.4 1.9 fusion.83
  (143 shorter events, 14.8 us)
Async XLA Ops:
  2.5 1.9 copy-start.9
  2.5 1.9 copy-start.18
  2.6 1.9 copy-start.19
  2.6 22.2 %copy-start.4 = (f32[128,256]{1,0:T(8,128)S(1)}, f32[128,256]{1,0:T(8,128)}, u32[]{:S(2)}) copy-start(f32[128,256]{1,0:T(8,128)} %param.21) | copy-start | bytes 393220
  2.6 22.2 %copy-start.5 = (f32[128,256]{1,0:T(8,128)S(1)}, f32[128,256]{1,0:T(8,128)}, u32[]{:S(2)}) copy-start(f32[128,256]{1,0:T(8,128)} %param.22) | copy-start | bytes 393220
  2.6 26.9 %copy-start.3 = (f32[4,128,128]{2,1,0:T(8,128)S(1)}, f32[4,128,128]{2,1,0:T(8,128)}, u32[]{:S(2)}) copy-start(f32[4,128,128]{2,1,0:T(8,128)} %param.26) | copy-start | bytes 786436
  4.5 25.0 %copy-start = (f32[4,128,128]{2,1,0:T(8,128)S(1)}, f32[4,128,128]{2,1,0:T(8,128)}, u32[]{:S(2)}) copy-start(f32[4,128,128]{2,1,0:T(8,128)} %param.24) | copy-start | bytes 786436
  4.5 25.0 %copy-start.2 = (f32[4,128,128]{2,1,0:T(8,128)S(1)}, f32[4,128,128]{2,1,0:T(8,128)}, u32[]{:S(2)}) copy-start(f32[4,128,128]{2,1,0:T(8,128)} %param.25) | copy-start | bytes 786436
  13.3 105.3 %all-to-all-start.2 = ((s32[128,1,32]{2,1,0:T(1,128)}), s32[128,1,32]{2,1,0:T(1,128)S(1)}, u32[]{:S(2)}, u32[]{:S(2)}) async-start(s32[128,1,32]{2,1,0:T(1,128)} %bitcast.6), calls=%async_computation.2 | async-start | bytes 131072 | tf_op jit(solution)/shard_map/all_to_all | solution.py:129
  24.8 138.5 %collective-permute-start = (f32[2,1,256]{2,1,0:T(1,128)S(1)}, f32[2,1,256]{2,1,0:T(1,128)S(1)}, u32[]{:S(2)}, u32[]{:S(2)}) collective-permute-start(f32[2,1,256]{2,1,0:T(1,128)S(1)} %get-tuple-element.130), channel_id=1, source_target_pairs={{0,8},{8,16},{16,24},{24,32},{32,40},{40,48},{48,56},{56,64},{64,7... | collective-permute-start | bytes 6152 | tf_op jit(solution)/shard_map/ppermute | solution.py:17
  28.1 135.2 %collective-permute-start.1 = (f32[2,1,256]{2,1,0:T(1,128)S(1)}, f32[2,1,256]{2,1,0:T(1,128)S(1)}, u32[]{:S(2)}, u32[]{:S(2)}) collective-permute-start(f32[2,1,256]{2,1,0:T(1,128)S(1)} %get-tuple-element.131), channel_id=1, source_target_pairs={{8,0},{16,8},{24,16},{32,24},{40,32},{48,40},{56,48},{64,56},{72,6... | collective-permute-start | bytes 6152 | tf_op jit(solution)/shard_map/ppermute | solution.py:19
  29.7 0.7 copy-start.8
  31.1 3.7 copy-start.10
  35.5 54.5 %copy-start.11 = (s32[4096]{0:T(1024)S(1)}, s32[4096]{0:T(1024)}, u32[]{:S(2)}) copy-start(s32[4096]{0:T(1024)} %param.30) | copy-start | bytes 49156
  35.5 54.5 %copy-start.12 = (s32[4096]{0:T(1024)S(1)}, s32[4096]{0:T(1024)}, u32[]{:S(2)}) copy-start(s32[4096]{0:T(1024)} %param.29) | copy-start | bytes 49156
  58.6 31.5 %copy-start.20 = (s32[2048]{0:T(1024)S(1)}, s32[2048]{0:T(1024)}, u32[]{:S(2)}) copy-start(s32[2048]{0:T(1024)} %param.33) | copy-start | bytes 24580
  58.6 31.5 %copy-start.21 = (s32[2048]{0:T(1024)S(1)}, s32[2048]{0:T(1024)}, u32[]{:S(2)}) copy-start(s32[2048]{0:T(1024)} %param.32) | copy-start | bytes 24580
  90.1 273.4 %copy-start.22 = (s32[2048]{0:T(1024)}, s32[2048]{0:T(1024)S(1)}, u32[]{:S(2)}) copy-start(s32[2048]{0:T(1024)S(1)} %compare_select_fusion.5) | copy-start | bytes 24580
  90.1 17.1 %copy-start.7 = (f32[2048]{0:T(1024)S(1)}, f32[2048]{0:T(1024)}, u32[]{:S(2)}) copy-start(f32[2048]{0:T(1024)} %param.37) | copy-start | bytes 24580
  118.6 34.9 %all-to-all-start = ((s32[1,128,64]{2,0,1:T(1,128)}), s32[1,128,64]{2,0,1:T(1,128)S(1)}, u32[]{:S(2)}, u32[]{:S(2)}) async-start(s32[1,128,64]{2,0,1:T(1,128)} %bitcast.1), calls=%async_computation | async-start | bytes 131072 | tf_op jit(solution)/shard_map/all_to_all | solution.py:96
  153.5 19.1 %all-to-all-start.3 = ((f32[128,1,32]{2,1,0:T(1,128)}), f32[128,1,32]{2,1,0:T(1,128)S(1)}, u32[]{:S(2)}, u32[]{:S(2)}) async-start(f32[128,1,32]{2,1,0:T(1,128)} %bitcast.8), calls=%async_computation.3 | async-start | bytes 131072 | tf_op jit(solution)/shard_map/all_to_all | solution.py:147
  163.3 0.8 copy-start.14
  163.3 0.8 copy-start.16
  172.6 29.2 %all-to-all-start.1 = ((f32[128,1,128]{2,1,0:T(1,128)}), f32[128,1,128]{2,1,0:T(1,128)S(1)}, u32[]{:S(2)}, u32[]{:S(2)}) async-start(f32[128,1,128]{2,1,0:T(1,128)} %reshape.450), calls=%async_computation.1 | async-start | bytes 131072 | tf_op jit(solution)/shard_map/all_to_all | solution.py:89
  332.4 18.4 %all-to-all-start.4 = ((f32[128,1,32]{2,1,0:T(1,128)}), f32[128,1,32]{2,1,0:T(1,128)S(1)}, u32[]{:S(2)}, u32[]{:S(2)}) async-start(f32[128,1,32]{2,1,0:T(1,128)} %bitcast.13), calls=%async_computation.4 | async-start | bytes 131072 | tf_op jit(solution)/shard_map/all_to_all | solution.py:147
  341.6 216.8 %collective-permute-start.2 = (f32[2,130,1]{2,1,0:T(8,128)S(1)}, f32[2,130,1]{2,1,0:T(8,128)}, u32[]{:S(2)}, u32[]{:S(2)}) collective-permute-start(f32[2,130,1]{2,1,0:T(8,128)S(1)} %get-tuple-element.128), channel_id=1, source_target_pairs={{0,1},{1,2},{2,3},{3,4},{4,5},{5,6},{6,7},{8,9},{9,10},{10,11},{11... | collective-permute-start | bytes 3128 | tf_op jit(solution)/shard_map/ppermute | solution.py:17
  345.2 213.2 %collective-permute-start.3 = (f32[2,130,1]{2,1,0:T(8,128)S(1)}, f32[2,130,1]{2,1,0:T(8,128)}, u32[]{:S(2)}, u32[]{:S(2)}) collective-permute-start(f32[2,130,1]{2,1,0:T(8,128)S(1)} %get-tuple-element.129), channel_id=1, source_target_pairs={{1,0},{2,1},{3,2},{4,3},{5,4},{6,5},{7,6},{9,8},{10,9},{11,10},{12... | collective-permute-start | bytes 3128 | tf_op jit(solution)/shard_map/ppermute | solution.py:19
  398.9 15.5 %all-to-all-start.5 = ((f32[128,1,32]{2,1,0:T(1,128)}), f32[128,1,32]{2,1,0:T(1,128)S(1)}, u32[]{:S(2)}, u32[]{:S(2)}) async-start(f32[128,1,32]{2,1,0:T(1,128)} %bitcast.16), calls=%async_computation.5 | async-start | bytes 131072 | tf_op jit(solution)/shard_map/all_to_all | solution.py:147
  439.1 45.6 %copy-start.1 = (f32[4,128,128]{2,1,0:T(8,128)}, f32[4,128,128]{2,1,0:T(8,128)S(1)}, u32[]{:S(2)}) copy-start(f32[4,128,128]{2,1,0:T(8,128)S(1)} %fusion.76) | copy-start | bytes 786436
  439.1 50.9 %copy-start.13 = (f32[4096]{0:T(1024)S(1)}, f32[4096]{0:T(1024)}, u32[]{:S(2)}) copy-start(f32[4096]{0:T(1024)} %param.31) | copy-start | bytes 49156
  485.4 26.8 %all-to-all-start.6 = ((f32[128,1,64]{2,1,0:T(1,128)}), f32[128,1,64]{2,1,0:T(1,128)S(1)}, u32[]{:S(2)}, u32[]{:S(2)}) async-start(f32[128,1,64]{2,1,0:T(1,128)} %bitcast.19), calls=%async_computation.6 | async-start | bytes 131072 | tf_op jit(solution)/shard_map/all_to_all | solution.py:162
  536.1 22.3 %copy-start.6 = (f32[128,256]{1,0:T(8,128)S(1)}, f32[128,256]{1,0:T(8,128)}, u32[]{:S(2)}) copy-start(f32[128,256]{1,0:T(8,128)} %param.23) | copy-start | bytes 393220
  536.1 22.3 %copy-start.15 = (f32[2,1,256]{2,1,0:T(1,128)S(1)}, f32[2,1,256]{2,1,0:T(1,128)}, u32[]{:S(2)}) copy-start(f32[2,1,256]{2,1,0:T(1,128)} %copy-done.14) | copy-start | bytes 6148
  536.1 22.3 %copy-start.17 = (f32[2,1,256]{2,1,0:T(1,128)S(1)}, f32[2,1,256]{2,1,0:T(1,128)}, u32[]{:S(2)}) copy-start(f32[2,1,256]{2,1,0:T(1,128)} %copy-done.16) | copy-start | bytes 6148
where the time goes:
time: 561 us; the launch traced here: 560 us
  local copies, waits for them, and re-layouts  260 us (46%)
  other arithmetic  206 us (37%)
  starting transfers between devices  66.8 us (12%)
  waiting for transfers between devices  21.3 us (4%)
    gather x3, local copies, waits for them, and re-layouts, shards(): answer = current.reshape(-1)[served]  69.1 us
    scatter-add x1, other arithmetic, shards(): jnp.zeros((frac_count * area,), jnp.float32).at[got_index]  52.3 us
    scatter-add x1, other arithmetic, shards(): source_rhs = jnp.zeros((frac_count * area,), jnp.float32).at[got_index].a...  52.3 us
    gather x1, local copies, waits for them, and re-layouts, shards(): reply = current.reshape(-1)[got_index]  45.5 us
    gather x3, local copies, waits for them, and re-layouts, shards(): partner = returned.reshape(-1)[junc_position]  35.3 us
    scatter-add x3, other arithmetic, shards(): jnp.zeros((frac_count * area,), jnp.float32).at[near_flat]  34.3 us
    all_to_all x3, starting transfers between devices, shards(): lax.all_to_all(answer, ('gx', 'gy'), split_axis=0, concat_axis=0, tiled=T...  24.9 us
    gather x1, local copies, waits for them, and re-layouts, shards(): matrix_pressure.reshape(-1)[isect_cell]  23 us
  transfers between devices with their start and end apart: 11, of which 3 were waited for; matrix products, arithmetic and copies ran while one was open for 58% of the time, Pallas kernels for 0%

commit v1 on v0

v1 whole, which is shorter than its diff:
```python
import jax
import jax.numpy as jnp
from jax import lax
from jax.experimental import pallas as pl
from jax.experimental.pallas import tpu as pltpu
from jax.sharding import PartitionSpec as P

LOGICAL = pl.DeviceIdType.LOGICAL
F32 = jnp.float32
BF16 = jnp.bfloat16
SWEEPS = 3
D = 128
QJ = 32
QI = 64


def dot_nn(a, b):
    return lax.dot_general(a, b, (((1,), (0,)), ((), ())), preferred_element_type=F32)


def dot_nt(a, b):
    return lax.dot_general(a, b, (((1,), (1,)), ((), ())), preferred_element_type=F32)


def halves(x):
    high = x.astype(BF16).astype(F32)
    return high, (x - high).astype(BF16).astype(F32)


def spread(row, rows):
    n = row.shape[1]
    block = jnp.broadcast_to(row, (16, n)).astype(BF16)
    return jnp.broadcast_to(block[None], (rows // 16, 16, n))


def counter(rows, n):
    return (
        (lax.broadcasted_iota(jnp.int32, (rows // 16, 16, n), 0) * 16
         + lax.broadcasted_iota(jnp.int32, (rows // 16, 16, n), 1)).astype(F32).astype(BF16)
    )


def hot(row, rows):
    n = row.shape[1]
    mask = counter(rows, n) == spread(row, rows)
    return jnp.where(mask, BF16(1), BF16(0)).reshape(rows, n)


def hot_values(row, values, rows):
    n = row.shape[1]
    mask = counter(rows, n) == spread(row, rows)
    return [
        jnp.where(mask, spread(v, rows), jnp.zeros((rows // 16, 16, n), BF16)).reshape(rows, n)
        for v in values
    ]


def hot512(row):
    return hot(row, 256), hot(row - 256.0, 256)


def divide(x, by):
    whole = jnp.floor(x * (1.0 / by))
    return whole, x - whole * by


def harmonic(first, second):
    return 2.0 * first * second / (first + second)


def kernel(
    mp, perm, stor, fp, ia, ns,
    icell, iown, ifrac, iseg, wi,
    jfrac, jseg, jown, jffrac, jfseg, jtrans,
    fnew, mnew,
    hot_own, hot_slot, col_hot, own_slot, own_q,
    tri, base,
    near_r, near_j, near_t, served_r, served_j, isr_r, isr_j, isr_w, isr_ws, cell_r, cell_c, cell_w,
    work, rhot_srv, rhot_near, rhot_is, rhot_cells, lv, tbl,
    q_now, cn, cs, cw, ce, inv, sto, apt, m_tot, m_wts,
    jsend, jrecv, isend, irecv, asend, arecv, rsend, rrecv, hsend, hrecv,
    send_sem, recv_sem, hsend_sem, hrecv_sem,
):
    gx = lax.axis_index("gx")
    gy = lax.axis_index("gy")
    me = gx * 8 + gy
    bar = pltpu.get_barrier_semaphore()

    def greet(k, c):
        pl.semaphore_signal(bar, inc=1, device_id=lax.rem(me + k, D), device_id_type=LOGICAL)
        return c

    lax.fori_loop(1, D, greet, 0)

    def exchange(number, src, dst, rows):
        def send(k, c):
            t = lax.rem(me + (D // 2) + k, D)
            pltpu.make_async_remote_copy(
                src.at[lax.rem(t, rows)], dst.at[me], send_sem.at[number], recv_sem.at[number],
                device_id=t, device_id_type=LOGICAL,
            ).start()
            return c

        lax.fori_loop(0, D // 2, send, 0)
        lax.fori_loop(D // 2 + 1, D, send, 0)
        pltpu.make_async_copy(src.at[lax.rem(me, rows)], dst.at[me], recv_sem.at[number]).start()

    def arrived(number, dst):
        pltpu.make_async_copy(dst, dst, recv_sem.at[number]).wait()

    def sent(number, dst):
        part = dst.at[pl.ds(0, D - 1)]
        pltpu.make_async_copy(part, part, send_sem.at[number]).wait()

    def merge(got, rows):
        blocks = D // rows
        width = D // blocks
        mine = me // rows
        lane_block = lax.broadcasted_iota(jnp.int32, (rows, D), 1) // width
        out = jnp.zeros((rows, D), F32)
        for k in range(blocks):
            part = pltpu.roll(got[k * rows:(k + 1) * rows, :], lax.rem((k - mine + blocks) * width, D), 1)
            out = jnp.where(lane_block == k, part, out)
        return out

    tri[...] = jnp.where(
        lax.broadcasted_iota(jnp.int32, (256, 256), 0) <= lax.broadcasted_iota(jnp.int32, (256, 256), 1), 1.0, 0.0
    ).astype(BF16)

    def slots(own_ref, count, rows, q_out, lane_out):
        width = rows
        base[...] = jnp.zeros((D, D), F32)

        def chunk(c, carry):
            for h in range(2):
                own = own_ref[pl.ds(2 * c + h, 1), :]
                mask = lax.broadcasted_iota(jnp.int32, (D, D), 0) == own
                hot_own[:, h * D:(h + 1) * D] = jnp.where(mask, 1.0, 0.0).astype(BF16)
            upto = dot_nn(hot_own[...], tri[...])
            before = base[...]
            for h in range(2):
                own = own_ref[pl.ds(2 * c + h, 1), :]
                mask = lax.broadcasted_iota(jnp.int32, (D, D), 0) == own
                rank = jnp.sum(jnp.where(mask, upto[:, h * D:(h + 1) * D] + before, 0.0), axis=0, keepdims=True) - 1.0
                block, rest = divide(own.astype(F32), rows)
                q_out[pl.ds(2 * c + h, 1), :] = rest
                lane_out[pl.ds(2 * c + h, 1), :] = block * width + rank
            base[...] = before + jnp.broadcast_to(upto[:, 255:256], (D, D))
            return carry

        lax.fori_loop(0, count // 2, chunk, 0)

    def pack(count, rows, values_of, planes):
        def chunk(c, carry):
            q = own_q[pl.ds(c, 1), :]
            at = pl.ds(pl.multiple_of(c * D, D), D)
            hot_slot[0:rows, at] = hot(q, rows)
            for p, v in enumerate(hot_values(own_slot[pl.ds(c, 1), :], values_of(c), D)):
                lv[p * D:(p + 1) * D, at] = v
            return carry

        lax.fori_loop(0, count, chunk, 0)
        out = dot_nt(hot_slot[0:rows, 0:count * D], lv[0:planes * D, 0:count * D])
        return [out[:, p * D:(p + 1) * D] for p in range(planes)]

    def gather(table, hots, j_ref, chunks, out):
        def chunk(c, carry):
            at = pl.ds(pl.multiple_of(c * 256, 256), 256)
            got = dot_nn(table[...], hots[:, at])
            both = got[0:D, :] + got[D:2 * D, :]
            for h in range(2):
                mask = lax.broadcasted_iota(jnp.int32, (D, D), 0) == j_ref[pl.ds(2 * c + h, 1), :].astype(jnp.int32)
                row = jnp.sum(jnp.where(mask, both[:, h * D:(h + 1) * D], 0.0), axis=0, keepdims=True)
                out(2 * c + h, row)
            return carry

        lax.fori_loop(0, chunks // 2, chunk, 0)

    def scatter(values, hots, j_ref, chunks):
        parts = 2 * len(values)

        def chunk(c, carry):
            at = pl.ds(pl.multiple_of(c * D, D), D)
            rows = []
            for v in values:
                rows.extend(halves(v[pl.ds(c, 1), :]))
            for p, v in enumerate(hot_values(j_ref[pl.ds(c, 1), :], rows, D)):
                lv[p * D:(p + 1) * D, at] = v
            return carry

        lax.fori_loop(0, chunks, chunk, 0)
        out = []
        for p in range(len(values)):
            both = dot_nt(lv[2 * p * D:(2 * p + 2) * D, 0:chunks * D], hots[...])
            out.append(both[0:D, :] + both[D:2 * D, :])
        return out

    def build512(r_ref, hots, chunks):
        def chunk(c, carry):
            at = pl.ds(pl.multiple_of(c * D, D), D)
            low, high = hot512(r_ref[pl.ds(c, 1), :])
            hots[0:256, at] = low
            hots[256:512, at] = high
            return carry

        lax.fori_loop(0, chunks, chunk, 0)

    def set_table(q):
        high, low = halves(q)
        tbl[0:D, :] = high.astype(BF16)
        tbl[D:2 * D, :] = low.astype(BF16)

    slots(jown, 16, QJ, own_q, own_slot)

    def requests(c):
        high, low = divide((jffrac[pl.ds(c, 1), :] * (D * D) + jfseg[pl.ds(c, 1), :]).astype(F32), 256)
        nigh, nlow = divide((jfrac[pl.ds(c, 1), :] * (D * D) + jseg[pl.ds(c, 1), :]).astype(F32), 256)
        t_high, t_low = halves(jtrans[pl.ds(c, 1), :])
        return [high * 256.0, low, nigh * 256.0, nlow, t_high, t_low]

    r_high, r_low, n_high, n_low, t_high, t_low = pack(16, QJ, requests, 6)
    jsend[:, 0, :] = r_high + r_low
    row, col = divide(n_high + n_low, D)
    near_r[...] = row
    near_j[...] = col
    near_t[...] = t_high + t_low
    pl.semaphore_wait(bar, D - 1)
    exchange(0, jsend, jrecv, QJ)

    p_high, p_low = halves(mp[...])
    work[0:D, :] = p_high.astype(BF16)
    work[D:2 * D, :] = p_low.astype(BF16)

    def cell_hots(c, carry):
        unused, col = divide(icell[pl.ds(c, 1), :].astype(F32), 256)
        col_hot[:, pl.ds(pl.multiple_of(c * D, D), D)] = hot(col, 256)
        cell_r[pl.ds(c, 1), :] = unused
        return carry

    lax.fori_loop(0, 32, cell_hots, 0)

    def keep_sample(c, row):
        isr_ws[pl.ds(c, 1), :] = row * wi[pl.ds(c, 1), :]

    gather(work, col_hot, cell_r, 32, keep_sample)
    slots(iown, 32, QI, own_q, own_slot)

    def wells(c):
        high, low = divide((ifrac[pl.ds(c, 1), :] * (D * D) + iseg[pl.ds(c, 1), :]).astype(F32), 256)
        c_high, c_low = divide(icell[pl.ds(c, 1), :].astype(F32), 256)
        w_high, w_low = halves(wi[pl.ds(c, 1), :])
        s_high, s_low = halves(isr_ws[pl.ds(c, 1), :])
        return [high * 256.0, low, w_high, w_low, s_high, s_low, c_high, c_low]

    i_high, i_low, w_high, w_low, s_high, s_low, c_high, c_low = pack(32, QI, wells, 8)
    isend[:, 0, 0, :] = i_high + i_low
    isend[:, 1, 0, :] = w_high + w_low
    isend[:, 2, 0, :] = s_high + s_low
    exchange(1, isend, irecv, QI)
    cell_r[...] = c_high
    cell_c[...] = c_low
    cell_w[...] = w_high + w_low

    for f in range(4):
        at = slice(f * D, (f + 1) * D)
        p0 = fp[f].T
        effective = ns[f].T - p0
        q_now[:, at] = p0
        apt[:, at] = ia[f].T - 0.5 * effective / (0.5 + effective)
    set_table(q_now[...])

    def answer(round_number):
        def keep(c, row):
            asend[round_number, pl.ds(c, 1), 0, :] = row

        gather(tbl, rhot_srv, served_j, QJ, keep)
        exchange(2 + round_number, asend.at[round_number], arecv.at[round_number], QJ)

    arrived(0, jrecv)
    row, col = divide(merge(jrecv[:, 0, :], QJ), D)
    served_r[...] = row
    served_j[...] = col
    build512(served_r, rhot_srv, QJ)
    answer(0)

    build512(near_r, rhot_near, QJ)
    (junc_diag,) = scatter([near_t], rhot_near, near_j, QJ)
    inv[...] = junc_diag
    arrived(1, irecv)
    row, col = divide(merge(irecv[:, 0, 0, :], QI), D)
    isr_r[...] = row
    isr_j[...] = col
    isr_w[...] = merge(irecv[:, 1, 0, :], QI)
    isr_ws[...] = merge(irecv[:, 2, 0, :], QI)
    build512(isr_r, rhot_is, QI)
    diag, rhs = scatter([isr_w, isr_ws], rhot_is, isr_j, QI)
    inv[...] += diag
    sto[...] = rhs
    lane = lax.broadcasted_iota(jnp.int32, (D, D), 1)
    sub = lax.broadcasted_iota(jnp.int32, (D, D), 0)
    for f in range(4):
        at = slice(f * D, (f + 1) * D)
        ap = apt[:, at]
        cond = ap * ap * ap
        north = jnp.where(lane == 0, 0.0, harmonic(cond, pltpu.roll(cond, 1, 1)))
        south = jnp.where(lane == D - 1, 0.0, harmonic(cond, pltpu.roll(cond, D - 1, 1)))
        west = jnp.where(sub == 0, 0.0, harmonic(cond, pltpu.roll(cond, 1, 0)))
        east = jnp.where(sub == D - 1, 0.0, harmonic(cond, pltpu.roll(cond, D - 1, 0)))
        one = 1.0 / (ap + north + south + west + east + inv[:, at])
        inv[:, at] = one
        cn[:, at] = north * one
        cs[:, at] = south * one
        cw[:, at] = west * one
        ce[:, at] = east * one
        sto[:, at] = (ap * q_now[:, at] + sto[:, at]) * one

    def sweep(round_number):
        arrived(2 + round_number, arecv.at[round_number])
        served_r[...] = merge(arecv[round_number, :, 0, :], QJ) * near_t[...]
        (joined,) = scatter([served_r], rhot_near, near_j, QJ)
        for f in range(4):
            at = slice(f * D, (f + 1) * D)
            q = q_now[:, at]
            q_now[:, at] = (
                sto[:, at]
                + cn[:, at] * pltpu.roll(q, 1, 1)
                + cs[:, at] * pltpu.roll(q, D - 1, 1)
                + cw[:, at] * pltpu.roll(q, 1, 0)
                + ce[:, at] * pltpu.roll(q, D - 1, 0)
                + inv[:, at] * joined[:, at]
            )
        set_table(q_now[...])

    sweep(0)
    answer(1)

    hsend[0, 0, 0, :] = mp[0, 0:D]
    hsend[0, 1, 0, :] = mp[0, D:2 * D]
    hsend[0, 2, 0, :] = perm[0, 0:D]
    hsend[0, 3, 0, :] = perm[0, D:2 * D]
    hsend[1, 0, 0, :] = mp[D - 1, 0:D]
    hsend[1, 1, 0, :] = mp[D - 1, D:2 * D]
    hsend[1, 2, 0, :] = perm[D - 1, 0:D]
    hsend[1, 3, 0, :] = perm[D - 1, D:2 * D]
    mp_left = mp[:, 0:D].T
    mp_right = mp[:, D:2 * D].T
    perm_left = perm[:, 0:D].T
    perm_right = perm[:, D:2 * D].T
    hsend[2, 0, 0, :] = mp_left[0, :]
    hsend[2, 2, 0, :] = perm_left[0, :]
    hsend[3, 0, 0, :] = mp_right[D - 1, :]
    hsend[3, 2, 0, :] = perm_right[D - 1, :]
    hsend[2, 1, 0, :] = mp_left[0, :]
    hsend[2, 3, 0, :] = perm_left[0, :]
    hsend[3, 1, 0, :] = mp_right[D - 1, :]
    hsend[3, 3, 0, :] = perm_right[D - 1, :]
    targets = (
        lax.rem(gx + 15, 16) * 8 + gy,
        lax.rem(gx + 1, 16) * 8 + gy,
        gx * 8 + lax.rem(gy + 7, 8),
        gx * 8 + lax.rem(gy + 1, 8),
    )
    halo = [
        pltpu.make_async_remote_copy(
            hsend.at[n], hrecv.at[n], hsend_sem.at[n], hrecv_sem.at[n], device_id=t, device_id_type=LOGICAL
        )
        for n, t in enumerate(targets)
    ]
    for copy in halo:
        copy.start()
    def cell_slots(c, carry):
        at = pl.ds(pl.multiple_of(c * D, D), D)
        rhot_cells[:, at] = hot(cell_c[pl.ds(c, 1), :], 256)
        return carry

    lax.fori_loop(0, QI, cell_slots, 0)
    (m_diag,) = scatter([cell_w], rhot_cells, cell_r, QI)
    m_wts[...] = stor[...] + m_diag

    sweep(1)
    answer(2)

    for copy in halo:
        copy.wait()
    press, k = mp[...], perm[...]
    rows = lax.broadcasted_iota(jnp.int32, (D, 256), 0)
    cols = lax.broadcasted_iota(jnp.int32, (D, 256), 1)

    def wide(n, plane):
        return jnp.concatenate([hrecv[n, plane], hrecv[n, plane + 1]], axis=1)

    def tall(n, plane):
        column = jnp.broadcast_to(hrecv[n, plane], (D, D)).T
        return jnp.concatenate([column, column], axis=1)

    total = stor[...] * press
    weights = m_wts[...]
    for n, shift, axis, at_edge, outside in (
        (1, 1, 0, rows == 0, gx == 0),
        (0, D - 1, 0, rows == D - 1, gx == 15),
        (3, 1, 1, cols == 0, gy == 0),
        (2, 255, 1, cols == 255, gy == 7),
    ):
        far_p = wide(n, 0) if axis == 0 else tall(n, 0)
        far_k = wide(n, 2) if axis == 0 else tall(n, 2)
        beside_p = jnp.where(at_edge, far_p, pltpu.roll(press, shift, axis))
        beside_k = jnp.where(at_edge, far_k, pltpu.roll(k, shift, axis))
        gone = jnp.where(outside, 0.0, 1.0)
        face = harmonic(k, beside_k) * jnp.where(at_edge, gone, 1.0)
        total = total + face * beside_p
        weights = weights + face
    m_tot[...] = total
    m_wts[...] = weights

    sweep(2)

    def keep_reply(c, row):
        rsend[pl.ds(c, 1), 0, :] = row

    gather(tbl, rhot_is, isr_j, QI, keep_reply)
    exchange(5, rsend, rrecv, QI)
    for f in range(4):
        fnew[f] = q_now[:, f * D:(f + 1) * D].T
    arrived(5, rrecv)
    isr_ws[...] = merge(rrecv[:, 0, :], QI) * cell_w[...]
    (m_rhs,) = scatter([isr_ws], rhot_cells, cell_r, QI)
    mnew[...] = (m_tot[...] + m_rhs) / m_wts[...]

    sent(0, jrecv)
    sent(1, irecv)
    for n in range(SWEEPS):
        sent(2 + n, arecv.at[n])
    sent(5, rrecv)


def shards(
    matrix_pressure, permeability, matrix_storage, fracture_pressure, initial_aperture, normal_stress,
    isect_cell, isect_owner, isect_frac, isect_seg, well_index,
    junc_frac, junc_seg, junc_owner, junc_far_frac, junc_far_seg, junc_trans,
):
    lanes = [
        a.reshape(-1, D)
        for a in (
            isect_cell, isect_owner, isect_frac, isect_seg, well_index,
            junc_frac, junc_seg, junc_owner, junc_far_frac, junc_far_seg, junc_trans,
        )
    ]
    vm = pltpu.VMEM
    scratch = [
        vm((D, 256), BF16),
        vm((QI, 4096), BF16),
        vm((256, 4096), BF16),
        vm((QI, D), F32),
        vm((QI, D), F32),
        vm((256, 256), BF16),
        vm((D, D), F32),
    ]
    scratch += [vm((QJ, D), F32)] * 5
    scratch += [vm((QI, D), F32)] * 7
    scratch += [
        vm((256, 256), BF16),
        vm((512, 4096), BF16),
        vm((512, 4096), BF16),
        vm((512, 8192), BF16),
        vm((256, 8192), BF16),
        vm((1024, 8192), BF16),
        vm((256, 512), BF16),
    ]
    scratch += [vm((D, 512), F32)] * 8
    scratch += [vm((D, 256), F32)] * 2
    scratch += [
        vm((QJ, 1, D), F32),
        vm((D, 1, D), F32),
        vm((QI, 3, 1, D), F32),
        vm((D, 3, 1, D), F32),
        vm((SWEEPS, QJ, 1, D), F32),
        vm((SWEEPS, D, 1, D), F32),
        vm((QI, 1, D), F32),
        vm((D, 1, D), F32),
        vm((4, 4, 1, D), F32),
        vm((4, 4, 1, D), F32),
        pltpu.SemaphoreType.DMA((6,)),
        pltpu.SemaphoreType.DMA((6,)),
        pltpu.SemaphoreType.DMA((4,)),
        pltpu.SemaphoreType.DMA((4,)),
    ]
    return pl.pallas_call(
        kernel,
        out_shape=(
            jax.ShapeDtypeStruct(fracture_pressure.shape, F32),
            jax.ShapeDtypeStruct(matrix_pressure.shape, F32),
        ),
        in_specs=[pl.BlockSpec(memory_space=pltpu.VMEM)] * 17,
        out_specs=(pl.BlockSpec(memory_space=pltpu.VMEM),) * 2,
        scratch_shapes=scratch,
        compiler_params=pltpu.CompilerParams(
            collective_id=0, has_side_effects=True, vmem_limit_bytes=60 << 20
        ),
    )(matrix_pressure, permeability, matrix_storage, fracture_pressure, initial_aperture, normal_stress, *lanes)


def solution(mesh):
    in_specs = (
        (P("gx", "gy"),) * 3
        + (P(("gx", "gy"), None, None),) * 3
        + (P(("gx", "gy")), P(("gx", "gy"), None), P(("gx", "gy")), P(("gx", "gy")), P(("gx", "gy")))
        + (P(("gx", "gy")), P(("gx", "gy")), P(("gx", "gy"), None), P(("gx", "gy")), P(("gx", "gy")), P(("gx", "gy")))
    )
    out_specs = (P(("gx", "gy"), None, None), P("gx", "gy"))
    return jax.shard_map(shards, mesh=mesh, in_specs=in_specs, out_specs=out_specs, check_vma=False)
```

time: 561 us -> 102 us (0.18)
  local copies, waits for them, and re-layouts: 260 us -> 2.36 us
  other arithmetic: 206 us -> 0 us
  Pallas kernels: 0 us -> 98.9 us
  starting transfers between devices: 66.8 us -> 0 us
  waiting for transfers between devices: 21.3 us -> 0 us
    gather x9 -> x0, local copies, waits for them, and re-layouts: 196 us -> none  [the longest x3 69.1 us: shards(): answer = current.reshape(-1)[served]]
    scatter-add x8 -> x0, other arithmetic: 194 us -> none  [the longest x1 52.3 us: shards(): jnp.zeros((frac_count * area,), jnp.float32).at[got_index]]
    pallas_call x0 -> x1, Pallas kernels: none -> 98.9 us  [shards(): pl.pallas_call(kernel, out_shape=(jax.ShapeDtypeStruct(fracture_pressure....]
    all_to_all x7 -> x0, starting transfers between devices: 56.7 us -> none  [the longest x3 24.9 us: shards(): lax.all_to_all(answer, ('gx', 'gy'), split_axis=0, concat_axis=0, tiled=T...]
    scatter x4 -> x0, local copies, waits for them, and re-layouts: 54.9 us -> none  [the longest x1 15.7 us: shards(): weight = jnp.zeros((slots_all,), jnp.float32).at[position].set(well_index)]
    all_to_all x7 -> x0, waiting for transfers between devices: 21.3 us -> none  [the longest x3 21.3 us: shards(): lax.all_to_all(answer, ('gx', 'gy'), split_axis=0, concat_axis=0, tiled=T...]
    ppermute x4 -> x0, starting transfers between devices: 10.2 us -> none  [the longest x2 6.95 us: padded_2(): lax.ppermute(tail, axis, [(i, (i + 1) % count) for i in range(ends)])]
  transfers between devices with their start and end apart: 11 -> 0, of which waited for: 3 -> 0; matrix products, arithmetic and copies ran while one was open for 58% -> 0% of each run, Pallas kernels for 0% -> 0%
where the time goes in v1:
time: 102 us
  Pallas kernels  98.9 us (97%)
  local copies, waits for them, and re-layouts  2.36 us (2%)
    pallas_call x1, Pallas kernels, shards(): pl.pallas_call(kernel, out_shape=(jax.ShapeDtypeStruct(fracture_pressure....  98.9 us
    unnamed x4, local copies, waits for them, and re-layouts  2.36 us

profile of v1, /device:TPU:1, one launch (start us, length us, event | category | flops | bytes accessed | tf_op | source)
XLA Modules:
  0.0 101.9 jit_solution(14452855107026981200)
XLA Ops:
  0.6 98.9 %shard_map.176 = (f32[4,128,128]{2,1,0:T(8,128)}, f32[128,256]{1,0:T(8,128)}) custom-call(f32[128,256]{1,0:T(8,128)} %mp.1, f32[128,256]{1,0:T(8,128)} %perm.1, f32[128,256]{1,0:T(8,128)} %stor.1, f32[4,128,128]{2,1,0:T(8,128)} %fp.1, f32[4,128,128]{2,1,0:T(8,128)} %ia.1, f32[4,128,128]{2,1,0:T(8,128)} %ns.1, s32[32,128]{1,0:T(8,128)} %bitcast.11, ...), custom_call_target="tpu_custom_call" | custom-call | tf_op jit(solution)/shard_map/pallas_call | solution.py:487
  99.6 0.0 copy-start
  99.6 1.7 %copy.21 = f32[4,128,128]{2,1,0:T(8,128)} copy(f32[4,128,128]{2,1,0:T(8,128)} %get-tuple-element.4) | data formatting | bytes 524288
  101.3 0.0 copy-done
  101.3 0.7 copy.22
Async XLA Ops:
  99.6 1.7 %copy-start = (f32[128,256]{1,0:T(8,128)S(1)}, f32[128,256]{1,0:T(8,128)}, u32[]{:S(2)}) copy-start(f32[128,256]{1,0:T(8,128)} %get-tuple-element.5) | copy-start | bytes 393220

commit v2 on v1

--- a/solution.py
+++ b/solution.py
@@ -68,15 +68,88 @@
     return 2.0 * first * second / (first + second)
 
 
+def slots(own_ref, count, rows, q_out, lane_out, hot_own, tri):
+    n = count * D
+
+    def build(c, carry):
+        at = pl.ds(pl.multiple_of(c * D, D), D)
+        hot_own[:, at] = hot(own_ref[pl.ds(c, 1), :].astype(F32), D)
+        return carry
+
+    lax.fori_loop(0, count, build, 0, unroll=4)
+    earlier = lax.broadcasted_iota(jnp.int32, (n, D), 0) // 256 < lax.broadcasted_iota(jnp.int32, (n, D), 1)
+    base = dot_nn(hot_own[:, 0:n], jnp.where(earlier, 1.0, 0.0).astype(BF16))
+    for c in range(count // 2):
+        upto = dot_nn(hot_own[:, c * 256:(c + 1) * 256], tri[...])
+        before = jnp.broadcast_to(base[:, c:c + 1], (D, D))
+        for h in range(2):
+            own = own_ref[2 * c + h:2 * c + h + 1, :]
+            mask = lax.broadcasted_iota(jnp.int32, (D, D), 0) == own
+            rank = jnp.sum(jnp.where(mask, upto[:, h * D:(h + 1) * D] + before, 0.0), axis=0, keepdims=True) - 1.0
+            block, rest = divide(own.astype(F32), rows)
+            q_out[2 * c + h:2 * c + h + 1, :] = rest
+            lane_out[2 * c + h:2 * c + h + 1, :] = block * rows + rank
+
+
+def pack(count, rows, values_of, planes, own_q, own_slot):
+    lanes, values = [], []
+    for c in range(count):
+        lanes.append(hot(own_slot[c:c + 1, :], D))
+        values.append(jnp.concatenate(hot_values(own_q[c:c + 1, :], values_of(c), rows), axis=0))
+    out = dot_nt(jnp.concatenate(values, axis=1), jnp.concatenate(lanes, axis=1))
+    return [out[p * rows:(p + 1) * rows, :] for p in range(planes)]
+
+
+def gather(table, hots, j_ref, chunks, out):
+    for c in range(chunks // 2):
+        got = dot_nn(table[...], hots[:, c * 256:(c + 1) * 256])
+        both = got[0:D, :] + got[D:2 * D, :]
+        for h in range(2):
+            k = 2 * c + h
+            mask = lax.broadcasted_iota(jnp.int32, (D, D), 0) == j_ref[k:k + 1, :].astype(jnp.int32)
+            out(k, jnp.sum(jnp.where(mask, both[:, h * D:(h + 1) * D], 0.0), axis=0, keepdims=True))
+
+
+def scatter(values, hots, j_ref, chunks, width=16):
+    total = None
+    for start in range(0, chunks, width):
+        parts = []
+        for c in range(start, start + width):
+            rows = []
+            for v in values:
+                rows.extend(halves(v[c:c + 1, :]))
+            parts.append(jnp.concatenate(hot_values(j_ref[c:c + 1, :], rows, D), axis=0))
+        part = dot_nt(jnp.concatenate(parts, axis=1), hots[:, start * D:(start + width) * D])
+        total = part if total is None else total + part
+    return [total[2 * p * D:(2 * p + 1) * D, :] + total[(2 * p + 1) * D:(2 * p + 2) * D, :] for p in range(len(values))]
+
+
+def build512(r_ref, hots, chunks):
+    def chunk(c, carry):
+        at = pl.ds(pl.multiple_of(c * D, D), D)
+        low, high = hot512(r_ref[pl.ds(c, 1), :])
+        hots[0:256, at] = low
+        hots[256:512, at] = high
+        return carry
+
+    lax.fori_loop(0, chunks, chunk, 0, unroll=4)
+
+
+def set_table(tbl, q):
+    high, low = halves(q)
+    tbl[0:D, :] = high.astype(BF16)
+    tbl[D:2 * D, :] = low.astype(BF16)
+
+
 def kernel(
     mp, perm, stor, fp, ia, ns,
     icell, iown, ifrac, iseg, wi,
     jfrac, jseg, jown, jffrac, jfseg, jtrans,
     fnew, mnew,
-    hot_own, hot_slot, col_hot, own_slot, own_q,
-    tri, base,
+    hot_own, col_hot, own_slot, own_q,
+    tri,
     near_r, near_j, near_t, served_r, served_j, isr_r, isr_j, isr_w, isr_ws, cell_r, cell_c, cell_w,
-    work, rhot_srv, rhot_near, rhot_is, rhot_cells, lv, tbl,
+    work, rhot_srv, rhot_near, rhot_is, rhot_cells, tbl,
     q_now, cn, cs, cw, ce, inv, sto, apt, m_tot, m_wts,
     jsend, jrecv, isend, irecv, asend, arecv, rsend, rrecv, hsend, hrecv,
     send_sem, recv_sem, hsend_sem, hrecv_sem,
@@ -127,98 +200,15 @@
         lax.broadcasted_iota(jnp.int32, (256, 256), 0) <= lax.broadcasted_iota(jnp.int32, (256, 256), 1), 1.0, 0.0
     ).astype(BF16)
 
-    def slots(own_ref, count, rows, q_out, lane_out):
-        width = rows
-        base[...] = jnp.zeros((D, D), F32)
-
-        def chunk(c, carry):
-            for h in range(2):
-                own = own_ref[pl.ds(2 * c + h, 1), :]
-                mask = lax.broadcasted_iota(jnp.int32, (D, D), 0) == own
-                hot_own[:, h * D:(h + 1) * D] = jnp.where(mask, 1.0, 0.0).astype(BF16)
-            upto = dot_nn(hot_own[...], tri[...])
-            before = base[...]
-            for h in range(2):
-                own = own_ref[pl.ds(2 * c + h, 1), :]
-                mask = lax.broadcasted_iota(jnp.int32, (D, D), 0) == own
-                rank = jnp.sum(jnp.where(mask, upto[:, h * D:(h + 1) * D] + before, 0.0), axis=0, keepdims=True) - 1.0
-                block, rest = divide(own.astype(F32), rows)
-                q_out[pl.ds(2 * c + h, 1), :] = rest
-                lane_out[pl.ds(2 * c + h, 1), :] = block * width + rank
-            base[...] = before + jnp.broadcast_to(upto[:, 255:256], (D, D))
-            return carry
-
-        lax.fori_loop(0, count // 2, chunk, 0)
-
-    def pack(count, rows, values_of, planes):
-        def chunk(c, carry):
-            q = own_q[pl.ds(c, 1), :]
-            at = pl.ds(pl.multiple_of(c * D, D), D)
-            hot_slot[0:rows, at] = hot(q, rows)
-            for p, v in enumerate(hot_values(own_slot[pl.ds(c, 1), :], values_of(c), D)):
-                lv[p * D:(p + 1) * D, at] = v
-            return carry
-
-        lax.fori_loop(0, count, chunk, 0)
-        out = dot_nt(hot_slot[0:rows, 0:count * D], lv[0:planes * D, 0:count * D])
-        return [out[:, p * D:(p + 1) * D] for p in range(planes)]
-
-    def gather(table, hots, j_ref, chunks, out):
-        def chunk(c, carry):
-            at = pl.ds(pl.multiple_of(c * 256, 256), 256)
-            got = dot_nn(table[...], hots[:, at])
-            both = got[0:D, :] + got[D:2 * D, :]
-            for h in range(2):
-                mask = lax.broadcasted_iota(jnp.int32, (D, D), 0) == j_ref[pl.ds(2 * c + h, 1), :].astype(jnp.int32)
-                row = jnp.sum(jnp.where(mask, both[:, h * D:(h + 1) * D], 0.0), axis=0, keepdims=True)
-                out(2 * c + h, row)
-            return carry
-
-        lax.fori_loop(0, chunks // 2, chunk, 0)
-
-    def scatter(values, hots, j_ref, chunks):
-        parts = 2 * len(values)
-
-        def chunk(c, carry):
-            at = pl.ds(pl.multiple_of(c * D, D), D)
-            rows = []
-            for v in values:
-                rows.extend(halves(v[pl.ds(c, 1), :]))
-            for p, v in enumerate(hot_values(j_ref[pl.ds(c, 1), :], rows, D)):
-                lv[p * D:(p + 1) * D, at] = v
-            return carry
-
-        lax.fori_loop(0, chunks, chunk, 0)
-        out = []
-        for p in range(len(values)):
-            both = dot_nt(lv[2 * p * D:(2 * p + 2) * D, 0:chunks * D], hots[...])
-            out.append(both[0:D, :] + both[D:2 * D, :])
-        return out
-
-    def build512(r_ref, hots, chunks):
-        def chunk(c, carry):
-            at = pl.ds(pl.multiple_of(c * D, D), D)
-            low, high = hot512(r_ref[pl.ds(c, 1), :])
-            hots[0:256, at] = low
-            hots[256:512, at] = high
-            return carry
-
-        lax.fori_loop(0, chunks, chunk, 0)
-
-    def set_table(q):
-        high, low = halves(q)
-        tbl[0:D, :] = high.astype(BF16)
-        tbl[D:2 * D, :] = low.astype(BF16)
-
-    slots(jown, 16, QJ, own_q, own_slot)
+    slots(jown, 16, QJ, own_q, own_slot, hot_own, tri)
 
     def requests(c):
-        high, low = divide((jffrac[pl.ds(c, 1), :] * (D * D) + jfseg[pl.ds(c, 1), :]).astype(F32), 256)
-        nigh, nlow = divide((jfrac[pl.ds(c, 1), :] * (D * D) + jseg[pl.ds(c, 1), :]).astype(F32), 256)
-        t_high, t_low = halves(jtrans[pl.ds(c, 1), :])
+        high, low = divide((jffrac[c:c + 1, :] * (D * D) + jfseg[c:c + 1, :]).astype(F32), 256)
+        nigh, nlow = divide((jfrac[c:c + 1, :] * (D * D) + jseg[c:c + 1, :]).astype(F32), 256)
+        t_high, t_low = halves(jtrans[c:c + 1, :])
         return [high * 256.0, low, nigh * 256.0, nlow, t_high, t_low]
 
-    r_high, r_low, n_high, n_low, t_high, t_low = pack(16, QJ, requests, 6)
+    r_high, r_low, n_high, n_low, t_high, t_low = pack(16, QJ, requests, 6, own_q, own_slot)
     jsend[:, 0, :] = r_high + r_low
     row, col = divide(n_high + n_low, D)
     near_r[...] = row
@@ -237,22 +227,22 @@
         cell_r[pl.ds(c, 1), :] = unused
         return carry
 
-    lax.fori_loop(0, 32, cell_hots, 0)
+    lax.fori_loop(0, 32, cell_hots, 0, unroll=4)
 
     def keep_sample(c, row):
-        isr_ws[pl.ds(c, 1), :] = row * wi[pl.ds(c, 1), :]
+        isr_ws[c:c + 1, :] = row * wi[c:c + 1, :]
 
     gather(work, col_hot, cell_r, 32, keep_sample)
-    slots(iown, 32, QI, own_q, own_slot)
+    slots(iown, 32, QI, own_q, own_slot, hot_own, tri)
 
     def wells(c):
-        high, low = divide((ifrac[pl.ds(c, 1), :] * (D * D) + iseg[pl.ds(c, 1), :]).astype(F32), 256)
-        c_high, c_low = divide(icell[pl.ds(c, 1), :].astype(F32), 256)
-        w_high, w_low = halves(wi[pl.ds(c, 1), :])
-        s_high, s_low = halves(isr_ws[pl.ds(c, 1), :])
+        high, low = divide((ifrac[c:c + 1, :] * (D * D) + iseg[c:c + 1, :]).astype(F32), 256)
+        c_high, c_low = divide(icell[c:c + 1, :].astype(F32), 256)
+        w_high, w_low = halves(wi[c:c + 1, :])
+        s_high, s_low = halves(isr_ws[c:c + 1, :])
         return [high * 256.0, low, w_high, w_low, s_high, s_low, c_high, c_low]
 
-    i_high, i_low, w_high, w_low, s_high, s_low, c_high, c_low = pack(32, QI, wells, 8)
+    i_high, i_low, w_high, w_low, s_high, s_low, c_high, c_low = pack(32, QI, wells, 8, own_q, own_slot)
     isend[:, 0, 0, :] = i_high + i_low
     isend[:, 1, 0, :] = w_high + w_low
     isend[:, 2, 0, :] = s_high + s_low
@@ -267,11 +257,11 @@
         effective = ns[f].T - p0
         q_now[:, at] = p0
         apt[:, at] = ia[f].T - 0.5 * effective / (0.5 + effective)
-    set_table(q_now[...])
+    set_table(tbl, q_now[...])
 
     def answer(round_number):
         def keep(c, row):
-            asend[round_number, pl.ds(c, 1), 0, :] = row
+            asend[round_number, c:c + 1, 0, :] = row
 
         gather(tbl, rhot_srv, served_j, QJ, keep)
         exchange(2 + round_number, asend.at[round_number], arecv.at[round_number], QJ)
@@ -329,7 +319,7 @@
                 + ce[:, at] * pltpu.roll(q, D - 1, 0)
                 + inv[:, at] * joined[:, at]
             )
-        set_table(q_now[...])
+        set_table(tbl, q_now[...])
 
     sweep(0)
     answer(1)
@@ -373,7 +363,7 @@
         rhot_cells[:, at] = hot(cell_c[pl.ds(c, 1), :], 256)
         return carry
 
-    lax.fori_loop(0, QI, cell_slots, 0)
+    lax.fori_loop(0, QI, cell_slots, 0, unroll=4)
     (m_diag,) = scatter([cell_w], rhot_cells, cell_r, QI)
     m_wts[...] = stor[...] + m_diag
 
@@ -415,7 +405,7 @@
     sweep(2)
 
     def keep_reply(c, row):
-        rsend[pl.ds(c, 1), 0, :] = row
+        rsend[c:c + 1, 0, :] = row
 
     gather(tbl, rhot_is, isr_j, QI, keep_reply)
     exchange(5, rsend, rrecv, QI)
@@ -447,13 +437,11 @@
     ]
     vm = pltpu.VMEM
     scratch = [
-        vm((D, 256), BF16),
-        vm((QI, 4096), BF16),
+        vm((D, 4096), BF16),
         vm((256, 4096), BF16),
         vm((QI, D), F32),
         vm((QI, D), F32),
         vm((256, 256), BF16),
-        vm((D, D), F32),
     ]
     scratch += [vm((QJ, D), F32)] * 5
     scratch += [vm((QI, D), F32)] * 7
@@ -463,7 +451,6 @@
         vm((512, 4096), BF16),
         vm((512, 8192), BF16),
         vm((256, 8192), BF16),
-        vm((1024, 8192), BF16),
         vm((256, 512), BF16),
     ]
     scratch += [vm((D, 512), F32)] * 8

time: 102 us -> 72.6 us (0.71)
  Pallas kernels: 98.9 us -> 69.5 us
    pallas_call x1, Pallas kernels: 98.9 us -> 69.5 us  [shards(): pl.pallas_call(kernel, out_shape=(jax.ShapeDtypeStruct(fracture_pressure....]
where the time goes in v2:
time: 72.6 us; the launch traced here: 72.5 us
  Pallas kernels  69.5 us (96%)
  local copies, waits for them, and re-layouts  2.36 us (3%)
    pallas_call x1, Pallas kernels, shards(): pl.pallas_call(kernel, out_shape=(jax.ShapeDtypeStruct(fracture_pressure....  69.5 us
    unnamed x4, local copies, waits for them, and re-layouts  2.36 us

profile of v2, /device:TPU:1, one launch (start us, length us, event | category | flops | bytes accessed | tf_op | source)
XLA Modules:
  0.0 72.5 jit_solution(16616953178981759140)
XLA Ops:
  0.6 69.5 %shard_map.176 = (f32[4,128,128]{2,1,0:T(8,128)}, f32[128,256]{1,0:T(8,128)}) custom-call(f32[128,256]{1,0:T(8,128)} %mp.1, f32[128,256]{1,0:T(8,128)} %perm.1, f32[128,256]{1,0:T(8,128)} %stor.1, f32[4,128,128]{2,1,0:T(8,128)} %fp.1, f32[4,128,128]{2,1,0:T(8,128)} %ia.1, f32[4,128,128]{2,1,0:T(8,128)} %ns.1, s32[32,128]{1,0:T(8,128)} %bitcast.11, ...), custom_call_target="tpu_custom_call" | custom-call | tf_op jit(solution)/shard_map/pallas_call | solution.py:474
  70.1 0.0 copy-start
  70.1 1.7 %copy.21 = f32[4,128,128]{2,1,0:T(8,128)} copy(f32[4,128,128]{2,1,0:T(8,128)} %get-tuple-element.4) | data formatting | bytes 524288
  71.8 0.0 copy-done
  71.8 0.7 copy.22
Async XLA Ops:
  70.1 1.7 %copy-start = (f32[128,256]{1,0:T(8,128)S(1)}, f32[128,256]{1,0:T(8,128)}, u32[]{:S(2)}) copy-start(f32[128,256]{1,0:T(8,128)} %get-tuple-element.5) | copy-start | bytes 393220

commit v3 on v2

--- a/solution.py
+++ b/solution.py
@@ -6,12 +6,23 @@
 from jax.sharding import PartitionSpec as P
 
 LOGICAL = pl.DeviceIdType.LOGICAL
+LOAD_ORDER = (13, 14, 15, 11, 12, 16, 6, 0, 7, 8, 9, 10, 3, 5, 4, 1, 2)
 F32 = jnp.float32
 BF16 = jnp.bfloat16
 SWEEPS = 3
 D = 128
 QJ = 32
 QI = 64
+
+
+def ring(d):
+    return min(d, 4 - d)
+
+
+ORDER = sorted(
+    [(dy, dx, dz, dc) for dy in range(4) for dx in range(4) for dz in range(4) for dc in range(2)][1:],
+    key=lambda v: -(ring(v[0]) + ring(v[1]) + ring(v[2])),
+)
 
 
 def dot_nn(a, b):
@@ -53,10 +64,6 @@
         jnp.where(mask, spread(v, rows), jnp.zeros((rows // 16, 16, n), BF16)).reshape(rows, n)
         for v in values
     ]
-
-
-def hot512(row):
-    return hot(row, 256), hot(row - 256.0, 256)
 
 
 def divide(x, by):
@@ -100,9 +107,22 @@
     return [out[p * rows:(p + 1) * rows, :] for p in range(planes)]
 
 
-def gather(table, hots, j_ref, chunks, out):
+def columns(row, rows):
+    if rows == 256:
+        return hot(row, 256)
+    return jnp.concatenate([hot(row, 256), hot(row - 256.0, 256)], axis=0)
+
+
+def gather(table, hots, j_ref, chunks, out, r_ref=None):
     for c in range(chunks // 2):
-        got = dot_nn(table[...], hots[:, c * 256:(c + 1) * 256])
+        at = slice(c * 256, (c + 1) * 256)
+        if r_ref is None:
+            cols = hots[:, at]
+        else:
+            cols = jnp.concatenate([columns(r_ref[k:k + 1, :], table.shape[1]) for k in (2 * c, 2 * c + 1)], axis=1)
+            if hots is not None:
+                hots[:, at] = cols
+        got = dot_nn(table[...], cols)
         both = got[0:D, :] + got[D:2 * D, :]
         for h in range(2):
             k = 2 * c + h
@@ -110,29 +130,26 @@
             out(k, jnp.sum(jnp.where(mask, both[:, h * D:(h + 1) * D], 0.0), axis=0, keepdims=True))
 
 
-def scatter(values, hots, j_ref, chunks, width=16):
+def scatter(values, hots, j_ref, chunks, r_ref=None, width=16):
     total = None
     for start in range(0, chunks, width):
-        parts = []
+        parts, made = [], []
+        at = slice(start * D, (start + width) * D)
         for c in range(start, start + width):
             rows = []
             for v in values:
                 rows.extend(halves(v[c:c + 1, :]))
             parts.append(jnp.concatenate(hot_values(j_ref[c:c + 1, :], rows, D), axis=0))
-        part = dot_nt(jnp.concatenate(parts, axis=1), hots[:, start * D:(start + width) * D])
+            if r_ref is not None:
+                made.append(columns(r_ref[c:c + 1, :], hots.shape[0]))
+        if r_ref is None:
+            cols = hots[:, at]
+        else:
+            cols = jnp.concatenate(made, axis=1)
+            hots[:, at] = cols
+        part = dot_nt(jnp.concatenate(parts, axis=1), cols)
         total = part if total is None else total + part
     return [total[2 * p * D:(2 * p + 1) * D, :] + total[(2 * p + 1) * D:(2 * p + 2) * D, :] for p in range(len(values))]
-
-
-def build512(r_ref, hots, chunks):
-    def chunk(c, carry):
-        at = pl.ds(pl.multiple_of(c * D, D), D)
-        low, high = hot512(r_ref[pl.ds(c, 1), :])
-        hots[0:256, at] = low
-        hots[256:512, at] = high
-        return carry
-
-    lax.fori_loop(0, chunks, chunk, 0, unroll=4)
 
 
 def set_table(tbl, q):
@@ -141,41 +158,47 @@
     tbl[D:2 * D, :] = low.astype(BF16)
 
 
-def kernel(
-    mp, perm, stor, fp, ia, ns,
-    icell, iown, ifrac, iseg, wi,
-    jfrac, jseg, jown, jffrac, jfseg, jtrans,
-    fnew, mnew,
-    hot_own, col_hot, own_slot, own_q,
-    tri,
-    near_r, near_j, near_t, served_r, served_j, isr_r, isr_j, isr_w, isr_ws, cell_r, cell_c, cell_w,
-    work, rhot_srv, rhot_near, rhot_is, rhot_cells, tbl,
-    q_now, cn, cs, cw, ce, inv, sto, apt, m_tot, m_wts,
-    jsend, jrecv, isend, irecv, asend, arecv, rsend, rrecv, hsend, hrecv,
-    send_sem, recv_sem, hsend_sem, hrecv_sem,
-):
+def kernel(*refs):
+    given, (fnew, mnew), held = refs[0:17], refs[17:19], refs[19:36]
+    (
+        mp, perm, stor, fp, ia, ns,
+        icell, iown, ifrac, iseg, wi,
+        jfrac, jseg, jown, jffrac, jfseg, jtrans,
+    ) = held
+    (
+        hot_own, own_slot, own_q, tri,
+        near_r, near_j, near_t, served_r, served_j, isr_r, isr_j, isr_w, isr_ws, cell_r, cell_c, cell_w,
+        work, rhot_srv, rhot_near, rhot_is, rhot_cells, tbl,
+        q_now, cn, cs, cw, ce, inv, sto, apt, m_tot, m_wts,
+        jsend, jrecv, isend, irecv, asend, arecv, rsend, rrecv, hsend, hrecv,
+        load_sem, send_sem, recv_sem, hsend_sem, hrecv_sem,
+    ) = refs[36:]
     gx = lax.axis_index("gx")
     gy = lax.axis_index("gy")
     me = gx * 8 + gy
+    y, x, z, core = gx // 4, lax.rem(gx, 4), gy // 2, lax.rem(gy, 2)
+
+    def peer(v):
+        return (lax.rem(y + v[0], 4) * 4 + lax.rem(x + v[1], 4)) * 8 + lax.rem(z + v[2], 4) * 2 + lax.rem(core + v[3], 2)
+
+    loads = [pltpu.make_async_copy(a, b, load_sem.at[n]) for n, (a, b) in enumerate(zip(given, held))]
+    for n in LOAD_ORDER:
+        loads[n].start()
     bar = pltpu.get_barrier_semaphore()
-
-    def greet(k, c):
-        pl.semaphore_signal(bar, inc=1, device_id=lax.rem(me + k, D), device_id_type=LOGICAL)
-        return c
-
-    lax.fori_loop(1, D, greet, 0)
+    for v in ORDER:
+        pl.semaphore_signal(bar, inc=1, device_id=peer(v), device_id_type=LOGICAL)
+
+    def ready(*numbers):
+        for n in numbers:
+            loads[n].wait()
 
     def exchange(number, src, dst, rows):
-        def send(k, c):
-            t = lax.rem(me + (D // 2) + k, D)
+        for v in ORDER:
+            t = peer(v)
             pltpu.make_async_remote_copy(
                 src.at[lax.rem(t, rows)], dst.at[me], send_sem.at[number], recv_sem.at[number],
                 device_id=t, device_id_type=LOGICAL,
             ).start()
-            return c
-
-        lax.fori_loop(0, D // 2, send, 0)
-        lax.fori_loop(D // 2 + 1, D, send, 0)
         pltpu.make_async_copy(src.at[lax.rem(me, rows)], dst.at[me], recv_sem.at[number]).start()
 
     def arrived(number, dst):
@@ -200,6 +223,7 @@
         lax.broadcasted_iota(jnp.int32, (256, 256), 0) <= lax.broadcasted_iota(jnp.int32, (256, 256), 1), 1.0, 0.0
     ).astype(BF16)
 
+    ready(13)
     slots(jown, 16, QJ, own_q, own_slot, hot_own, tri)
 
     def requests(c):
@@ -208,6 +232,7 @@
         t_high, t_low = halves(jtrans[c:c + 1, :])
         return [high * 256.0, low, nigh * 256.0, nlow, t_high, t_low]
 
+    ready(11, 12, 14, 15, 16)
     r_high, r_low, n_high, n_low, t_high, t_low = pack(16, QJ, requests, 6, own_q, own_slot)
     jsend[:, 0, :] = r_high + r_low
     row, col = divide(n_high + n_low, D)
@@ -217,22 +242,19 @@
     pl.semaphore_wait(bar, D - 1)
     exchange(0, jsend, jrecv, QJ)
 
+    ready(0, 6, 7, 8, 9, 10)
     p_high, p_low = halves(mp[...])
     work[0:D, :] = p_high.astype(BF16)
     work[D:2 * D, :] = p_low.astype(BF16)
 
-    def cell_hots(c, carry):
-        unused, col = divide(icell[pl.ds(c, 1), :].astype(F32), 256)
-        col_hot[:, pl.ds(pl.multiple_of(c * D, D), D)] = hot(col, 256)
-        cell_r[pl.ds(c, 1), :] = unused
-        return carry
-
-    lax.fori_loop(0, 32, cell_hots, 0, unroll=4)
+    row, col = divide(icell[...].astype(F32), 256)
+    cell_r[0:32, :] = row
+    cell_c[0:32, :] = col
 
     def keep_sample(c, row):
         isr_ws[c:c + 1, :] = row * wi[c:c + 1, :]
 
-    gather(work, col_hot, cell_r, 32, keep_sample)
+    gather(work, None, cell_r, 32, keep_sample, cell_c)
     slots(iown, 32, QI, own_q, own_slot, hot_own, tri)
 
     def wells(c):
@@ -251,6 +273,7 @@
     cell_c[...] = c_low
     cell_w[...] = w_high + w_low
 
+    ready(3, 4, 5)
     for f in range(4):
         at = slice(f * D, (f + 1) * D)
         p0 = fp[f].T
@@ -259,31 +282,29 @@
         apt[:, at] = ia[f].T - 0.5 * effective / (0.5 + effective)
     set_table(tbl, q_now[...])
 
+    (junc_diag,) = scatter([near_t], rhot_near, near_j, QJ, near_r)
+    inv[...] = junc_diag
+
     def answer(round_number):
         def keep(c, row):
             asend[round_number, c:c + 1, 0, :] = row
 
-        gather(tbl, rhot_srv, served_j, QJ, keep)
+        gather(tbl, rhot_srv, served_j, QJ, keep, served_r if round_number == 0 else None)
         exchange(2 + round_number, asend.at[round_number], arecv.at[round_number], QJ)
 
     arrived(0, jrecv)
     row, col = divide(merge(jrecv[:, 0, :], QJ), D)
     served_r[...] = row
     served_j[...] = col
-    build512(served_r, rhot_srv, QJ)
     answer(0)
 
-    build512(near_r, rhot_near, QJ)
-    (junc_diag,) = scatter([near_t], rhot_near, near_j, QJ)
-    inv[...] = junc_diag
     arrived(1, irecv)
     row, col = divide(merge(irecv[:, 0, 0, :], QI), D)
     isr_r[...] = row
     isr_j[...] = col
     isr_w[...] = merge(irecv[:, 1, 0, :], QI)
     isr_ws[...] = merge(irecv[:, 2, 0, :], QI)
-    build512(isr_r, rhot_is, QI)
-    diag, rhs = scatter([isr_w, isr_ws], rhot_is, isr_j, QI)
+    diag, rhs = scatter([isr_w, isr_ws], rhot_is, isr_j, QI, isr_r)
     inv[...] += diag
     sto[...] = rhs
     lane = lax.broadcasted_iota(jnp.int32, (D, D), 1)
@@ -324,6 +345,7 @@
     sweep(0)
     answer(1)
 
+    ready(1, 2)
     hsend[0, 0, 0, :] = mp[0, 0:D]
     hsend[0, 1, 0, :] = mp[0, D:2 * D]
     hsend[0, 2, 0, :] = perm[0, 0:D]
@@ -358,13 +380,7 @@
     ]
     for copy in halo:
         copy.start()
-    def cell_slots(c, carry):
-        at = pl.ds(pl.multiple_of(c * D, D), D)
-        rhot_cells[:, at] = hot(cell_c[pl.ds(c, 1), :], 256)
-        return carry
-
-    lax.fori_loop(0, QI, cell_slots, 0, unroll=4)
-    (m_diag,) = scatter([cell_w], rhot_cells, cell_r, QI)
+    (m_diag,) = scatter([cell_w], rhot_cells, cell_r, QI, cell_c)
     m_wts[...] = stor[...] + m_diag
 
     sweep(1)
@@ -423,6 +439,11 @@
     sent(5, rrecv)
 
 
+def hand_over(a, b, a_out, b_out):
+    a_out[...] = a[...]
+    b_out[...] = b[...]
+
+
 def shards(
     matrix_pressure, permeability, matrix_storage, fracture_pressure, initial_aperture, normal_stress,
     isect_cell, isect_owner, isect_frac, isect_seg, well_index,
@@ -436,9 +457,10 @@
         )
     ]
     vm = pltpu.VMEM
-    scratch = [
+    args = (matrix_pressure, permeability, matrix_storage, fracture_pressure, initial_aperture, normal_stress, *lanes)
+    scratch = [vm(a.shape, a.dtype) for a in args]
+    scratch += [
         vm((D, 4096), BF16),
-        vm((256, 4096), BF16),
         vm((QI, D), F32),
         vm((QI, D), F32),
         vm((256, 256), BF16),
@@ -466,24 +488,26 @@
         vm((D, 1, D), F32),
         vm((4, 4, 1, D), F32),
         vm((4, 4, 1, D), F32),
+        pltpu.SemaphoreType.DMA((17,)),
         pltpu.SemaphoreType.DMA((6,)),
         pltpu.SemaphoreType.DMA((6,)),
         pltpu.SemaphoreType.DMA((4,)),
         pltpu.SemaphoreType.DMA((4,)),
     ]
-    return pl.pallas_call(
+    shapes = (
+        jax.ShapeDtypeStruct(fracture_pressure.shape, F32),
+        jax.ShapeDtypeStruct(matrix_pressure.shape, F32),
+    )
+    results = pl.pallas_call(
         kernel,
-        out_shape=(
-            jax.ShapeDtypeStruct(fracture_pressure.shape, F32),
-            jax.ShapeDtypeStruct(matrix_pressure.shape, F32),
-        ),
-        in_specs=[pl.BlockSpec(memory_space=pltpu.VMEM)] * 17,
+        out_shape=shapes,
+        in_specs=[pl.BlockSpec(memory_space=pltpu.HBM)] * 17,
         out_specs=(pl.BlockSpec(memory_space=pltpu.VMEM),) * 2,
         scratch_shapes=scratch,
-        compiler_params=pltpu.CompilerParams(
-            collective_id=0, has_side_effects=True, vmem_limit_bytes=60 << 20
-        ),
-    )(matrix_pressure, permeability, matrix_storage, fracture_pressure, initial_aperture, normal_stress, *lanes)
+        compiler_params=pltpu.CompilerParams(collective_id=0, has_side_effects=True, vmem_limit_bytes=63 << 20),
+    )(*args)
+    whole = pl.BlockSpec(memory_space=pltpu.VMEM)
+    return pl.pallas_call(hand_over, out_shape=shapes, in_specs=[whole] * 2, out_specs=(whole,) * 2)(*results)
 
 
 def solution(mesh):

time: 72.6 us -> 65 us (0.90)
  Pallas kernels: 69.5 us -> 64.2 us
  local copies, waits for them, and re-layouts: 2.36 us -> 0 us
    pallas_call x1 -> x2, Pallas kernels: 69.5 us -> 64.2 us  [the longest x1 62.5 us: shards(): pl.pallas_call(kernel, out_shape=shapes, in_specs=[pl.BlockSpec(memory_sp...]
    unnamed x4 -> x0, local copies, waits for them, and re-layouts: 2.36 us -> none
where the time goes in v3:
time: 65 us; the launch traced here: 64.9 us
  Pallas kernels  64.2 us (99%)
  between operations  0.65 us (1%)
    pallas_call x1, Pallas kernels, shards(): pl.pallas_call(kernel, out_shape=shapes, in_specs=[pl.BlockSpec(memory_sp...  62.5 us
    pallas_call x1, Pallas kernels, shards(): pl.pallas_call(hand_over, out_shape=shapes, in_specs=[whole] * 2, out_spe...  1.74 us

profile of v3, /device:TPU:1, one launch (start us, length us, event | category | flops | bytes accessed | tf_op | source)
XLA Modules:
  0.0 64.9 jit_solution(5064248183184698222)
XLA Ops:
  0.6 62.5 %shard_map.176 = (f32[4,128,128]{2,1,0:T(8,128)}, f32[128,256]{1,0:T(8,128)}) custom-call(f32[128,256]{1,0:T(8,128)} %refs_0_.1, f32[128,256]{1,0:T(8,128)} %refs_1_.1, f32[128,256]{1,0:T(8,128)} %refs_2_.1, f32[4,128,128]{2,1,0:T(8,128)} %refs_3_.1, f32[4,128,128]{2,1,0:T(8,128)} %refs_4_.1, f32[4,128,128]{2,1,0:T(8,128)} %refs_5_.1, s32[32,128]{1,0:T(8,128)} %bitcast.11, ...), custom_call_target="tpu_custom_call" | custom-call | tf_op jit(solution)/shard_map/pallas_call | solution.py:501
  63.1 1.7 %shard_map.177 = (f32[4,128,128]{2,1,0:T(8,128)}, f32[128,256]{1,0:T(8,128)}) custom-call(f32[4,128,128]{2,1,0:T(8,128)} %get-tuple-element.4.a, f32[128,256]{1,0:T(8,128)} %get-tuple-element.5.b), custom_call_target="tpu_custom_call" | custom-call | tf_op jit(solution)/shard_map/pallas_call | solution.py:510

commit v4 on v3

--- a/solution.py
+++ b/solution.py
@@ -6,6 +6,7 @@
 from jax.sharding import PartitionSpec as P
 
 LOGICAL = pl.DeviceIdType.LOGICAL
+STEPS_X = (2, 1, 3, 0)
 LOAD_ORDER = (13, 14, 15, 11, 12, 16, 6, 0, 7, 8, 9, 10, 3, 5, 4, 1, 2)
 F32 = jnp.float32
 BF16 = jnp.bfloat16
@@ -113,43 +114,53 @@
     return jnp.concatenate([hot(row, 256), hot(row - 256.0, 256)], axis=0)
 
 
-def gather(table, hots, j_ref, chunks, out, r_ref=None):
-    for c in range(chunks // 2):
-        at = slice(c * 256, (c + 1) * 256)
-        if r_ref is None:
-            cols = hots[:, at]
-        else:
-            cols = jnp.concatenate([columns(r_ref[k:k + 1, :], table.shape[1]) for k in (2 * c, 2 * c + 1)], axis=1)
-            if hots is not None:
-                hots[:, at] = cols
-        got = dot_nn(table[...], cols)
-        both = got[0:D, :] + got[D:2 * D, :]
-        for h in range(2):
-            k = 2 * c + h
-            mask = lax.broadcasted_iota(jnp.int32, (D, D), 0) == j_ref[k:k + 1, :].astype(jnp.int32)
-            out(k, jnp.sum(jnp.where(mask, both[:, h * D:(h + 1) * D], 0.0), axis=0, keepdims=True))
+def gather(table, hots, j_ref, starts, out, r_ref=None):
+    for start in starts:
+        js = j_ref[pl.ds(start, 8), :].astype(jnp.int32)
+        rs = None if r_ref is None else r_ref[pl.ds(start, 8), :]
+        for c in range(4):
+            at = pl.ds(pl.multiple_of(start * D + c * 256, 256), 256)
+            if r_ref is None:
+                cols = hots[:, at]
+            else:
+                cols = jnp.concatenate([columns(rs[k:k + 1, :], table.shape[1]) for k in (2 * c, 2 * c + 1)], axis=1)
+                if hots is not None:
+                    hots[:, at] = cols
+            got = dot_nn(table[...], cols)
+            both = got[0:D, :] + got[D:2 * D, :]
+            for h in range(2):
+                k = 2 * c + h
+                mask = lax.broadcasted_iota(jnp.int32, (D, D), 0) == js[k:k + 1, :]
+                out(start + k, jnp.sum(jnp.where(mask, both[:, h * D:(h + 1) * D], 0.0), axis=0, keepdims=True))
+
+
+def scatter_block(values, hots, j_ref, start, r_ref=None):
+    n = values[0].shape[0]
+    js = j_ref[pl.ds(start, n), :]
+    at = pl.ds(pl.multiple_of(start * D, D), n * D)
+    parts, made = [], []
+    split = [part for v in values for part in halves(v)]
+    for c in range(n):
+        parts.append(jnp.concatenate(hot_values(js[c:c + 1, :], [v[c:c + 1, :] for v in split], D), axis=0))
+    if r_ref is None:
+        cols = hots[:, at]
+    else:
+        rs = r_ref[pl.ds(start, n), :]
+        cols = jnp.concatenate([columns(rs[c:c + 1, :], hots.shape[0]) for c in range(n)], axis=1)
+        hots[:, at] = cols
+    return dot_nt(jnp.concatenate(parts, axis=1), cols)
+
+
+def add_halves(total, count):
+    return [total[2 * p * D:(2 * p + 1) * D, :] + total[(2 * p + 1) * D:(2 * p + 2) * D, :] for p in range(count)]
 
 
 def scatter(values, hots, j_ref, chunks, r_ref=None, width=16):
     total = None
     for start in range(0, chunks, width):
-        parts, made = [], []
-        at = slice(start * D, (start + width) * D)
-        for c in range(start, start + width):
-            rows = []
-            for v in values:
-                rows.extend(halves(v[c:c + 1, :]))
-            parts.append(jnp.concatenate(hot_values(j_ref[c:c + 1, :], rows, D), axis=0))
-            if r_ref is not None:
-                made.append(columns(r_ref[c:c + 1, :], hots.shape[0]))
-        if r_ref is None:
-            cols = hots[:, at]
-        else:
-            cols = jnp.concatenate(made, axis=1)
-            hots[:, at] = cols
-        part = dot_nt(jnp.concatenate(parts, axis=1), cols)
+        part = scatter_block([v[start:start + width, :] for v in values], hots, j_ref, start, r_ref)
         total = part if total is None else total + part
-    return [total[2 * p * D:(2 * p + 1) * D, :] + total[(2 * p + 1) * D:(2 * p + 2) * D, :] for p in range(len(values))]
+    return add_halves(total, len(values))
 
 
 def set_table(tbl, q):
@@ -192,30 +203,37 @@
         for n in numbers:
             loads[n].wait()
 
-    def exchange(number, src, dst, rows):
-        for v in ORDER:
-            t = peer(v)
-            pltpu.make_async_remote_copy(
-                src.at[lax.rem(t, rows)], dst.at[me], send_sem.at[number], recv_sem.at[number],
-                device_id=t, device_id_type=LOGICAL,
-            ).start()
-        pltpu.make_async_copy(src.at[lax.rem(me, rows)], dst.at[me], recv_sem.at[number]).start()
-
-    def arrived(number, dst):
-        pltpu.make_async_copy(dst, dst, recv_sem.at[number]).wait()
+    def exchange(number, src, dst, rows, steps=STEPS_X):
+        for dx in steps:
+            for v in ORDER:
+                if v[1] == dx:
+                    t = peer(v)
+                    pltpu.make_async_remote_copy(
+                        src.at[lax.rem(t, rows)], dst.at[me], send_sem.at[number], recv_sem.at[number, dx],
+                        device_id=t, device_id_type=LOGICAL,
+                    ).start()
+            if dx == 0:
+                pltpu.make_async_copy(src.at[lax.rem(me, rows)], dst.at[me], recv_sem.at[number, dx]).start()
+
+    def arrived(number, dst, dx):
+        part = dst.at[pl.ds(0, 32)]
+        pltpu.make_async_copy(part, part, recv_sem.at[number, dx]).wait()
 
     def sent(number, dst):
         part = dst.at[pl.ds(0, D - 1)]
         pltpu.make_async_copy(part, part, send_sem.at[number]).wait()
 
-    def merge(got, rows):
+    def first_row(step):
+        return pl.multiple_of(lax.rem(x + step, 4) * 8, 8)
+
+    def merge(read, rows, start=0, count=None):
+        count = rows if count is None else count
         blocks = D // rows
         width = D // blocks
-        mine = me // rows
-        lane_block = lax.broadcasted_iota(jnp.int32, (rows, D), 1) // width
-        out = jnp.zeros((rows, D), F32)
+        lane_block = lax.broadcasted_iota(jnp.int32, (count, D), 1) // width
+        out = jnp.zeros((count, D), F32)
         for k in range(blocks):
-            part = pltpu.roll(got[k * rows:(k + 1) * rows, :], lax.rem((k - mine + blocks) * width, D), 1)
+            part = pltpu.roll(read(k * rows + start, count), lax.rem((k - me // rows + blocks) * width, D), 1)
             out = jnp.where(lane_block == k, part, out)
         return out
 
@@ -239,8 +257,6 @@
     near_r[...] = row
     near_j[...] = col
     near_t[...] = t_high + t_low
-    pl.semaphore_wait(bar, D - 1)
-    exchange(0, jsend, jrecv, QJ)
 
     ready(0, 6, 7, 8, 9, 10)
     p_high, p_low = halves(mp[...])
@@ -254,8 +270,10 @@
     def keep_sample(c, row):
         isr_ws[c:c + 1, :] = row * wi[c:c + 1, :]
 
-    gather(work, None, cell_r, 32, keep_sample, cell_c)
+    gather(work, None, cell_r, range(0, 32, 8), keep_sample, cell_c)
     slots(iown, 32, QI, own_q, own_slot, hot_own, tri)
+    pl.semaphore_wait(bar, D - 1)
+    exchange(0, jsend, jrecv, QJ)
 
     def wells(c):
         high, low = divide((ifrac[c:c + 1, :] * (D * D) + iseg[c:c + 1, :]).astype(F32), 256)
@@ -285,25 +303,33 @@
     (junc_diag,) = scatter([near_t], rhot_near, near_j, QJ, near_r)
     inv[...] = junc_diag
 
+    def keep_answer(round_number):
+        def keep(c, row):
+            asend[round_number, pl.ds(c, 1), 0, :] = row
+
+        return keep
+
     def answer(round_number):
-        def keep(c, row):
-            asend[round_number, c:c + 1, 0, :] = row
-
-        gather(tbl, rhot_srv, served_j, QJ, keep, served_r if round_number == 0 else None)
-        exchange(2 + round_number, asend.at[round_number], arecv.at[round_number], QJ)
-
-    arrived(0, jrecv)
-    row, col = divide(merge(jrecv[:, 0, :], QJ), D)
-    served_r[...] = row
-    served_j[...] = col
-    answer(0)
-
-    arrived(1, irecv)
-    row, col = divide(merge(irecv[:, 0, 0, :], QI), D)
+        for dx in STEPS_X:
+            gather(tbl, rhot_srv, served_j, [first_row(dx)], keep_answer(round_number))
+            exchange(2 + round_number, asend.at[round_number], arecv.at[round_number], QJ, (dx,))
+
+    for dx in STEPS_X:
+        arrived(0, jrecv, dx)
+        start = first_row(4 - dx)
+        row, col = divide(merge(lambda at, n: jrecv[pl.ds(at, n), 0, :], QJ, start, 8), D)
+        served_r[pl.ds(start, 8), :] = row
+        served_j[pl.ds(start, 8), :] = col
+        gather(tbl, rhot_srv, served_j, [start], keep_answer(0), served_r)
+        exchange(2, asend.at[0], arecv.at[0], QJ, ((4 - dx) % 4,))
+
+    for dx in STEPS_X:
+        arrived(1, irecv, dx)
+    row, col = divide(merge(lambda at, n: irecv[at:at + n, 0, 0, :], QI), D)
     isr_r[...] = row
     isr_j[...] = col
-    isr_w[...] = merge(irecv[:, 1, 0, :], QI)
-    isr_ws[...] = merge(irecv[:, 2, 0, :], QI)
+    isr_w[...] = merge(lambda at, n: irecv[at:at + n, 1, 0, :], QI)
+    isr_ws[...] = merge(lambda at, n: irecv[at:at + n, 2, 0, :], QI)
     diag, rhs = scatter([isr_w, isr_ws], rhot_is, isr_j, QI, isr_r)
     inv[...] += diag
     sto[...] = rhs
@@ -326,9 +352,14 @@
         sto[:, at] = (ap * q_now[:, at] + sto[:, at]) * one
 
     def sweep(round_number):
-        arrived(2 + round_number, arecv.at[round_number])
-        served_r[...] = merge(arecv[round_number, :, 0, :], QJ) * near_t[...]
-        (joined,) = scatter([served_r], rhot_near, near_j, QJ)
+        total = None
+        for dx in STEPS_X:
+            arrived(2 + round_number, arecv.at[round_number], dx)
+            start = first_row(4 - dx)
+            got = merge(lambda at, n: arecv[round_number, pl.ds(at, n), 0, :], QJ, start, 8)
+            part = scatter_block([got * near_t[pl.ds(start, 8), :]], rhot_near, near_j, start)
+            total = part if total is None else total + part
+        (joined,) = add_halves(total, 1)
         for f in range(4):
             at = slice(f * D, (f + 1) * D)
             q = q_now[:, at]
@@ -421,15 +452,23 @@
     sweep(2)
 
     def keep_reply(c, row):
-        rsend[c:c + 1, 0, :] = row
-
-    gather(tbl, rhot_is, isr_j, QI, keep_reply)
-    exchange(5, rsend, rrecv, QI)
+        rsend[pl.ds(c, 1), 0, :] = row
+
+    for dx in STEPS_X:
+        start = first_row(dx)
+        gather(tbl, rhot_is, isr_j, [start, pl.multiple_of(start + 32, 8)], keep_reply)
+        exchange(5, rsend, rrecv, QI, (dx,))
     for f in range(4):
         fnew[f] = q_now[:, f * D:(f + 1) * D].T
-    arrived(5, rrecv)
-    isr_ws[...] = merge(rrecv[:, 0, :], QI) * cell_w[...]
-    (m_rhs,) = scatter([isr_ws], rhot_cells, cell_r, QI)
+    total = None
+    for dx in STEPS_X:
+        arrived(5, rrecv, dx)
+        for more in (0, 32):
+            start = pl.multiple_of(first_row(4 - dx) + more, 8)
+            got = merge(lambda at, n: rrecv[pl.ds(at, n), 0, :], QI, start, 8)
+            part = scatter_block([got * cell_w[pl.ds(start, 8), :]], rhot_cells, cell_r, start)
+            total = part if total is None else total + part
+    (m_rhs,) = add_halves(total, 1)
     mnew[...] = (m_tot[...] + m_rhs) / m_wts[...]
 
     sent(0, jrecv)
@@ -490,7 +529,7 @@
         vm((4, 4, 1, D), F32),
         pltpu.SemaphoreType.DMA((17,)),
         pltpu.SemaphoreType.DMA((6,)),
-        pltpu.SemaphoreType.DMA((6,)),
+        pltpu.SemaphoreType.DMA((6, 4)),
         pltpu.SemaphoreType.DMA((4,)),
         pltpu.SemaphoreType.DMA((4,)),
     ]

time: 65 us -> 61.7 us (0.949)
  Pallas kernels: 64.2 us -> 60.9 us
    pallas_call x1, Pallas kernels: 62.5 us -> 59.2 us  [shards(): pl.pallas_call(kernel, out_shape=shapes, in_specs=[pl.BlockSpec(memory_sp...]
where the time goes in v4:
time: 61.7 us; the launch traced here: 61.6 us
  Pallas kernels  60.9 us (99%)
  between operations  0.65 us (1%)
    pallas_call x1, Pallas kernels, shards(): pl.pallas_call(kernel, out_shape=shapes, in_specs=[pl.BlockSpec(memory_sp...  59.2 us
    pallas_call x1, Pallas kernels, shards(): pl.pallas_call(hand_over, out_shape=shapes, in_specs=[whole] * 2, out_spe...  1.74 us

profile of v4, /device:TPU:1, one launch (start us, length us, event | category | flops | bytes accessed | tf_op | source)
XLA Modules:
  0.0 61.6 jit_solution(6095069631222528540)
XLA Ops:
  0.6 59.2 %shard_map.176 = (f32[4,128,128]{2,1,0:T(8,128)}, f32[128,256]{1,0:T(8,128)}) custom-call(f32[128,256]{1,0:T(8,128)} %refs_0_.1, f32[128,256]{1,0:T(8,128)} %refs_1_.1, f32[128,256]{1,0:T(8,128)} %refs_2_.1, f32[4,128,128]{2,1,0:T(8,128)} %refs_3_.1, f32[4,128,128]{2,1,0:T(8,128)} %refs_4_.1, f32[4,128,128]{2,1,0:T(8,128)} %refs_5_.1, s32[32,128]{1,0:T(8,128)} %bitcast.11, ...), custom_call_target="tpu_custom_call" | custom-call | tf_op jit(solution)/shard_map/pallas_call | solution.py:540
  59.8 1.7 %shard_map.177 = (f32[4,128,128]{2,1,0:T(8,128)}, f32[128,256]{1,0:T(8,128)}) custom-call(f32[4,128,128]{2,1,0:T(8,128)} %get-tuple-element.4.a, f32[128,256]{1,0:T(8,128)} %get-tuple-element.5.b), custom_call_target="tpu_custom_call" | custom-call | tf_op jit(solution)/shard_map/pallas_call | solution.py:549

commit v5 on v4

--- a/solution.py
+++ b/solution.py
@@ -189,8 +189,17 @@
     me = gx * 8 + gy
     y, x, z, core = gx // 4, lax.rem(gx, 4), gy // 2, lax.rem(gy, 2)
 
+    half = [lax.rem(y + d, 2) * 32 for d in range(2)]
+    x_part = [lax.rem(x + d, 4) * 8 for d in range(4)]
+    yx_part = [[lax.rem(y + e, 4) * 32 + x_part[d] for d in range(4)] for e in range(4)]
+    low_part = [[lax.rem(z + d, 4) * 2 + lax.rem(core + e, 2) for e in range(2)] for d in range(4)]
+    hx_part = [[half[e] + x_part[d] for d in range(4)] for e in range(2)]
+
     def peer(v):
-        return (lax.rem(y + v[0], 4) * 4 + lax.rem(x + v[1], 4)) * 8 + lax.rem(z + v[2], 4) * 2 + lax.rem(core + v[3], 2)
+        return yx_part[v[0]][v[1]] + low_part[v[2]][v[3]]
+
+    def slot_row(v, rows):
+        return (x_part[v[1]] if rows == QJ else hx_part[v[0] % 2][v[1]]) + low_part[v[2]][v[3]]
 
     loads = [pltpu.make_async_copy(a, b, load_sem.at[n]) for n, (a, b) in enumerate(zip(given, held))]
     for n in LOAD_ORDER:
@@ -209,7 +218,7 @@
                 if v[1] == dx:
                     t = peer(v)
                     pltpu.make_async_remote_copy(
-                        src.at[lax.rem(t, rows)], dst.at[me], send_sem.at[number], recv_sem.at[number, dx],
+                        src.at[slot_row(v, rows)], dst.at[me], send_sem.at[number], recv_sem.at[number, dx],
                         device_id=t, device_id_type=LOGICAL,
                     ).start()
             if dx == 0:
@@ -272,6 +281,8 @@
 
     gather(work, None, cell_r, range(0, 32, 8), keep_sample, cell_c)
     slots(iown, 32, QI, own_q, own_slot, hot_own, tri)
+    (junc_diag,) = scatter([near_t], rhot_near, near_j, QJ, near_r)
+    inv[...] = junc_diag
     pl.semaphore_wait(bar, D - 1)
     exchange(0, jsend, jrecv, QJ)
 
@@ -300,8 +311,6 @@
         apt[:, at] = ia[f].T - 0.5 * effective / (0.5 + effective)
     set_table(tbl, q_now[...])
 
-    (junc_diag,) = scatter([near_t], rhot_near, near_j, QJ, near_r)
-    inv[...] = junc_diag
 
     def keep_answer(round_number):
         def keep(c, row):

time: 61.7 us -> 57.6 us (0.934)
  Pallas kernels: 60.9 us -> 56.9 us
    pallas_call x1, Pallas kernels: 59.2 us -> 55.1 us  [shards(): pl.pallas_call(kernel, out_shape=shapes, in_specs=[pl.BlockSpec(memory_sp...]
where the time goes in v5:
time: 57.6 us; the launch traced here: 57.5 us
  Pallas kernels  56.9 us (99%)
  between operations  0.65 us (1%)
    pallas_call x1, Pallas kernels, shards(): pl.pallas_call(kernel, out_shape=shapes, in_specs=[pl.BlockSpec(memory_sp...  55.1 us
    pallas_call x1, Pallas kernels, shards(): pl.pallas_call(hand_over, out_shape=shapes, in_specs=[whole] * 2, out_spe...  1.74 us

profile of v5, /device:TPU:1, one launch (start us, length us, event | category | flops | bytes accessed | tf_op | source)
XLA Modules:
  0.0 57.5 jit_solution(11445166110222494716)
XLA Ops:
  0.6 55.1 %shard_map.176 = (f32[4,128,128]{2,1,0:T(8,128)}, f32[128,256]{1,0:T(8,128)}) custom-call(f32[128,256]{1,0:T(8,128)} %refs_0_.1, f32[128,256]{1,0:T(8,128)} %refs_1_.1, f32[128,256]{1,0:T(8,128)} %refs_2_.1, f32[4,128,128]{2,1,0:T(8,128)} %refs_3_.1, f32[4,128,128]{2,1,0:T(8,128)} %refs_4_.1, f32[4,128,128]{2,1,0:T(8,128)} %refs_5_.1, s32[32,128]{1,0:T(8,128)} %bitcast.11, ...), custom_call_target="tpu_custom_call" | custom-call | tf_op jit(solution)/shard_map/pallas_call | solution.py:549
  55.8 1.7 %shard_map.177 = (f32[4,128,128]{2,1,0:T(8,128)}, f32[128,256]{1,0:T(8,128)}) custom-call(f32[4,128,128]{2,1,0:T(8,128)} %get-tuple-element.4.a, f32[128,256]{1,0:T(8,128)} %get-tuple-element.5.b), custom_call_target="tpu_custom_call" | custom-call | tf_op jit(solution)/shard_map/pallas_call | solution.py:558
